TPU v7x, 256 devices: a whole 4x4x8 slice. The times are simulated.
256 devices in a mesh: head: 16 (over z, core), tail: 16 (over y, x).
Axes of the slice: x: 4, y: 4, z: 8, core: 2. Of those that a mesh axis runs over, the one named last changes fastest.
Arguments:
- head_emb: bfloat16 [131072, 800], P(('head', 'tail')), may hold values from -48 to 48
- head_state: float32 [131072], P(('head', 'tail')), may hold values from 0.01 to 1
- tail_emb: bfloat16 [64, 128, 800], P('tail'), may hold values from -1.5 to 1.5
- tail_state: float32 [64, 128], P('tail'), may hold values from 0.01 to 1
- relation_emb: bfloat16 [1024, 800], replicated, may hold values from -3.5 to 3.5
- head_rows: int32 [1024, 256], P(('head', 'tail')), may hold values from 0 to 511
- relations: int32 [1024, 256], P(('head', 'tail')), may hold values from 0 to 1023
- tail_offsets: int32 [1024, 256], P(('head', 'tail')), may hold values from 0 to 127
- tail_owner: int32 [1024, 1], P(('head', 'tail')), may hold values from 0 to 15; in each aligned block of 4 rows (0 to 3, 4 to 7, ...) at most 2 rows name the same one
- tail_local: int32 [1024], P(('head', 'tail')), may hold values from 0 to 3
- block_count: int32 [256], P(('head', 'tail')), may hold values from 1 to 4, as said below
- neg_blocks: int32 [8], replicated, may hold values from 0 to 63, as said below
Outputs:
- head_new: bfloat16 [131072, 800], P(('head', 'tail'))
- head_state_new: float32 [131072], P(('head', 'tail'))
- tail_new: bfloat16 [64, 128, 800], P('tail')
- tail_state_new: float32 [64, 128], P('tail')
Inputs may be any that keep to these rules, and one draw needn't show every extreme that they name: `tail_owner`: no tail index owns the tail blocks of more than 2 edge block slots of one device, and in some devices one owns exactly 2. `block_count`: some device has all 4 slots live. `neg_blocks`: distinct tail blocks; the last tail block is always among them.
All inputs are finite; a program needn't handle non-finite values.
Results may differ from a plain program's by a relative error of at most 0.0012.
The roundings to bfloat16 on the way count: a program that leaves them out, or rounds other values in their place, can miss the bound.
Values may be sent and summed in bfloat16 or wider, within the bound.
A program may use at most 128 MiB of HBM per device.

v0:
```python
import math

import jax
import jax.numpy as jnp
from jax import lax
from jax.sharding import PartitionSpec as P

LEARN_RATE = 0.3


def complex_product(left, right):
    half_width = left.shape[-1] // 2
    left_re, left_im = (left[..., :half_width], left[..., half_width:])
    right_re, right_im = (right[..., :half_width], right[..., half_width:])
    return jnp.concatenate(
        [left_re * right_re - left_im * right_im, left_re * right_im + left_im * right_re], axis=-1
    )


def conj_product(left, right):
    half_width = left.shape[-1] // 2
    left_re, left_im = (left[..., :half_width], left[..., half_width:])
    right_re, right_im = (right[..., :half_width], right[..., half_width:])
    return jnp.concatenate(
        [left_re * right_re + left_im * right_im, left_im * right_re - left_re * right_im], axis=-1
    )


def row_adagrad(embedding, adagrad_state, gradient):
    state_next = adagrad_state + jnp.mean(gradient * gradient, axis=-1)
    updated = (
        embedding.astype(jnp.float32) - LEARN_RATE * gradient / jnp.sqrt(state_next)[..., None]
    )
    return (updated.astype(jnp.bfloat16), state_next)


def head_sum(tail_grad):
    return lax.psum(tail_grad, "head")


def per_device(
    head_emb,
    head_state,
    tail_emb,
    tail_state,
    relation_emb,
    head_rows,
    relations,
    tail_offsets,
    tail_owner,
    tail_local,
    block_count,
    neg_blocks,
):
    block_total = tail_local.shape[0]
    edge_count = head_rows.shape[1]
    row_width = head_emb.shape[1]
    span_rows = tail_emb.shape[1]
    owned_blocks = tail_emb.shape[0]
    peer_count = lax.axis_size("tail")
    tail_rank = lax.axis_index("tail")
    capacity = max(2, (2 * block_total + peer_count - 1) // peer_count)
    owner_rank = tail_owner[:, 0]
    positions = jnp.arange(block_total, dtype=jnp.int32)
    same_owner = owner_rank[:, None] == owner_rank[None, :]
    earlier = positions[None, :] < positions[:, None]
    slot_index = jnp.sum((same_owner & earlier).astype(jnp.int32), axis=1)
    slot_place = owner_rank * capacity + slot_index
    global_block = owner_rank * owned_blocks + tail_local
    partition = lax.all_gather(tail_emb, "tail", axis=0, tiled=True)
    chosen = jnp.take(partition, global_block, axis=0)
    mine_ids = neg_blocks - tail_rank * owned_blocks
    is_mine = (mine_ids >= 0) & (mine_ids < owned_blocks)
    own_negs = jnp.where(
        is_mine[:, None, None],
        jnp.take(tail_emb, jnp.clip(mine_ids, 0, owned_blocks - 1), axis=0),
        jnp.zeros((), jnp.bfloat16),
    )
    negatives = lax.psum(own_negs.astype(jnp.float32).astype(jnp.bfloat16), "tail").reshape(
        -1, row_width
    )
    total_edges = block_total * edge_count
    flat_rows = head_rows.reshape(-1)
    block_of = jnp.arange(total_edges, dtype=jnp.int32) // edge_count
    live_mask = (block_of < block_count[0]).astype(jnp.float32)
    tail_index = block_of * span_rows + tail_offsets.reshape(-1)
    tail_vectors = jnp.take(chosen.reshape(-1, row_width), tail_index, axis=0)
    relation_vectors = jnp.take(relation_emb, relations.reshape(-1), axis=0)
    head_vectors = jnp.take(head_emb, flat_rows, axis=0)
    query = complex_product(
        head_vectors.astype(jnp.float32), relation_vectors.astype(jnp.float32)
    ).astype(jnp.bfloat16)
    per_group = math.gcd(block_total, max(1, 512 // edge_count))
    group_rows = per_group * edge_count
    group_count = total_edges // group_rows

    def grouped(values):
        return values.reshape((group_count, group_rows) + values.shape[1:])

    def score_group(neg_total, group_items):
        query_rows, tail_rows, live_rows = group_items
        query_float = query_rows.astype(jnp.float32)
        positive = jnp.sum(query_float * tail_rows.astype(jnp.float32), axis=1)
        negative = lax.dot_general(
            query_rows, negatives, (((1,), (1,)), ((), ())), preferred_element_type=jnp.float32
        )
        largest = jnp.maximum(positive, jnp.max(negative, axis=1))
        pos_exp = jnp.exp(positive - largest)
        neg_exp = jnp.exp(negative - largest[:, None])
        denominator = pos_exp + jnp.sum(neg_exp, axis=1)
        pos_grad = (pos_exp / denominator - 1.0) * live_rows
        neg_grad = (neg_exp / denominator[:, None] * live_rows[:, None]).astype(jnp.bfloat16)
        query_grad = pos_grad[:, None] * tail_rows.astype(jnp.float32) + jnp.dot(
            neg_grad, negatives, preferred_element_type=jnp.float32
        )
        tail_part = pos_grad[:, None] * query_float
        neg_total = neg_total + lax.dot_general(
            neg_grad, query_rows, (((0,), (0,)), ((), ())), preferred_element_type=jnp.float32
        )
        return (neg_total, (query_grad, tail_part))

    neg_start = jnp.zeros((negatives.shape[0], row_width), jnp.float32)
    neg_part, (query_grad, tail_part) = lax.scan(
        score_group, neg_start, (grouped(query), grouped(tail_vectors), grouped(live_mask))
    )
    query_grad = query_grad.reshape(total_edges, row_width)
    tail_part = tail_part.reshape(total_edges, row_width)
    head_grad = (
        jnp.zeros(head_emb.shape, jnp.float32)
        .at[flat_rows]
        .add(conj_product(query_grad, relation_vectors.astype(jnp.float32)))
    )
    block_grad = (
        jnp.zeros((block_total * span_rows, row_width), jnp.float32)
        .at[tail_index]
        .add(tail_part)
        .astype(jnp.bfloat16)
    )
    outgoing = (
        jnp.zeros((peer_count * capacity, span_rows, row_width), jnp.bfloat16)
        .at[slot_place]
        .set(block_grad.reshape(block_total, span_rows, row_width))
    )
    outgoing = outgoing.reshape(peer_count, capacity, span_rows, row_width)
    slot_ids = (
        jnp.zeros((peer_count * capacity,), jnp.int32)
        .at[slot_place]
        .set(tail_local)
        .reshape(peer_count, capacity)
    )
    incoming, incoming_ids = (
        lax.all_to_all(outgoing, "tail", split_axis=0, concat_axis=0, tiled=True),
        lax.all_to_all(slot_ids, "tail", split_axis=0, concat_axis=0, tiled=True),
    )
    which_block = (
        incoming_ids.reshape(-1)[:, None] == jnp.arange(owned_blocks, dtype=jnp.int32)[None, :]
    ).astype(jnp.bfloat16)
    tail_grad = lax.dot_general(
        which_block,
        incoming.reshape(peer_count * capacity, span_rows * row_width),
        (((0,), (0,)), ((), ())),
        preferred_element_type=jnp.float32,
    )
    neg_weights = (
        (mine_ids[:, None] == jnp.arange(owned_blocks, dtype=jnp.int32)[None, :]) & is_mine[:, None]
    ).astype(jnp.float32)
    neg_all = lax.psum(neg_part, ("head", "tail"))
    tail_total = head_sum(tail_grad) + lax.dot_general(
        neg_weights,
        neg_all.reshape(neg_weights.shape[0], span_rows * row_width),
        (((0,), (0,)), ((), ())),
        precision=lax.Precision.HIGHEST,
        preferred_element_type=jnp.float32,
    )
    head_updated, head_state_updated = row_adagrad(head_emb, head_state, head_grad)
    tail_updated, tail_state_updated = row_adagrad(
        tail_emb, tail_state, tail_total.reshape(owned_blocks, span_rows, row_width)
    )
    return (head_updated, head_state_updated, tail_updated, tail_state_updated)


def solution(mesh):
    placed = (
        P(("head", "tail"), None),
        P(("head", "tail")),
        P("tail", None, None),
        P("tail", None),
        P(),
        P(("head", "tail"), None),
        P(("head", "tail"), None),
        P(("head", "tail"), None),
        P(("head", "tail"), None),
        P(("head", "tail")),
        P(("head", "tail")),
        P(),
    )
    return jax.shard_map(
        per_device,
        mesh=mesh,
        in_specs=placed,
        out_specs=(
            P(("head", "tail"), None),
            P(("head", "tail")),
            P("tail", None, None),
            P("tail", None),
        ),
        check_vma=False,
    )
```

profile of v0, /device:TPU:1, one launch (start us, length us, event | category | flops | bytes accessed | tf_op | source)
XLA Modules:
  0.0 728.6 jit_solution(752198037437776522)
XLA Ops:
  10.9 7.6 %all-to-all-start = ((s32[16,1,2]{2,1,0:T(1,128)}), s32[16,1,2]{2,1,0:T(1,128)S(1)}, u32[]{:S(2)}, u32[]{:S(2)}) async-start(s32[16,1,2]{2,1,0:T(1,128)} %bitcast.13), calls=%async_computation | async-start | bytes 16384 | tf_op jit(solution)/shard_map/all_to_all | solution.py:153
  21.6 3.8 copy.82
  26.1 3.1 copy.79
  29.3 5.3 gather_fusion.3
  34.6 5.3 gather_fusion
  48.7 63.1 %all-gather.2.cloned.1.call-done = bf16[64,128,800]{1,2,0:T(8,128)(2,1)} async-done(((bf16[4,128,800]{1,2,0:T(8,128)(2,1)}), bf16[64,128,800]{1,2,0:T(8,128)(2,1)}) %all-gather.2.cloned.1.call-update) | async-done | bytes 13107216 | tf_op jit(solution)/shard_map/all_gather | solution.py:70
  111.9 5.4 gather_fusion.2
  119.9 5.3 gather_fusion.4
  125.2 3.2 broadcast_select_fusion
  128.4 3.5 copy.84
  131.9 81.2 %all-reduce.4.cloned.1.call-done = bf16[1024,800]{1,0:T(8,128)(2,1)} async-done(((bf16[1024,800]{1,0:T(8,128)(2,1)}), bf16[1024,800]{1,0:T(8,128)(2,1)}) %all-reduce.4.cloned.1.call-update) | async-done | bytes 1638416 | tf_op jit(solution)/shard_map/psum | solution.py:79
  213.2 30.7 %while.17 = (s32[]{:T(128)}, f32[1024,800]{0,1:T(8,128)}, f32[2,512,800]{1,2,0:T(8,128)}, f32[2,512,800]{1,2,0:T(8,128)}, bf16[2,512,800]{1,2,0:T(8,128)(2,1)S(1...) while((s32[]{:T(128)}, f32[1024,800]{0,1:T(8,128)}, ...), condition=%wide.region_5.7_spmd.clone, body=%wide.region_1.6_spmd.clone.sunk | while | flops 2527675904 | bytes 74365712 | solution.py:123
  213.2 3.0 fusion.55
  223.6 4.5 select_add_fusion.2
  238.4 5.4 select_add_fusion.2
  243.9 4.4 copy.95
  248.2 10.8 %scatter_custom_fusion.2 = f32[512,800]{1,0:T(8,128)S(1)} fusion(s32[1024]{0:T(1024)S(1)} %bitcast.112, f32[1024,800]{1,0:T(8,128)} %bitcast.92, f32[]{:T(128)} %constant.133.clone.1), kind=kCustom, calls=%fused_computation.49 | custom fusion | flops 819200 | bytes 1638912 | tf_op jit(solution)/shard_map/scatter-add | solution.py:136
  261.7 3.6 broadcast_in_dim.108
  268.1 4.6 all-to-all-start.1
  272.8 4.9 copy.92
  277.6 6.1 reshape.276
  287.4 4.4 copy.85
  291.8 76.1 %all-to-all-done.1 = bf16[16,2,128,800]{2,3,1,0:T(8,128)(2,1)} async-done(((bf16[16,2,128,800]{2,3,1,0:T(8,128)(2,1)}), bf16[16,2,128,800]{2,3,1,0:T(8,128)(2,1)}, u32[]{:S(2)}, u32[]{:S(2)}) %all-to-all-start.1) | async-done | bytes 6553632 | tf_op jit(solution)/shard_map/all_to_all | solution.py:152
  367.9 11.0 %copy.91 = bf16[16,2,128,800]{3,2,1,0:T(8,128)(2,1)} copy(bf16[16,2,128,800]{2,3,1,0:T(8,128)(2,1)} %all-to-all-done.1) | data formatting | bytes 13107200 | tf_op jit(solution)/shard_map/all_to_all | solution.py:152
  379.0 13.6 %reshape.275 = bf16[32,102400]{1,0:T(8,128)(2,1)} reshape(bf16[16,2,128,800]{3,2,1,0:T(8,128)(2,1)} %copy.91) | data formatting | bytes 13107200 | tf_op jit(solution)/shard_map/reshape | solution.py:160
  392.6 5.1 fusion.20
  397.8 6.6 multiply_add_fusion
  404.4 10.9 %scatter_custom_fusion = f32[512,800]{1,0:T(8,128)S(1)} fusion(s32[1024]{0:T(1024)S(1)} %bitcast.113, f32[1024,400]{1,0:T(8,128)} %get-tuple-element.225, f32[]{:T(128)} %constant.164, f32[1024,400]{1,0:T(8,128)} %get-tuple-element.224, f32[]{:T(128)} %constant.133.clone.1), kind=kCustom, calls=%fused_computation.32 | custom fusion | flops 1638400 | bytes 4915208 | tf_op jit(solution)/shard_map/scatter-add | solution.py:131
  419.6 171.0 %all-reduce.8.cloned.1.call-done = f32[8,102400]{1,0:T(8,128)} async-done(((f32[8,102400]{1,0:T(8,128)}), f32[8,102400]{1,0:T(8,128)}) %all-reduce.8.cloned.1.call-update) | async-done | bytes 3276816 | tf_op jit(solution)/shard_map/psum | solution.py:167
  590.6 116.0 %all-reduce.6.cloned.1.call-done = f32[4,102400]{1,0:T(4,128)} async-done(((f32[4,102400]{1,0:T(4,128)}), f32[4,102400]{1,0:T(4,128)}) %all-reduce.6.cloned.1.call-update) | async-done | bytes 1638416 | tf_op jit(solution)/shard_map/psum | solution.py:38
  706.6 5.1 broadcast_multiply_fusion
  714.9 3.1 mul.157
  (125 shorter events, 56.5 us)
Async XLA Ops:
  7.2 12.1 %copy-start.3 = (bf16[4,128,800]{1,2,0:T(8,128)(2,1)S(1)}, bf16[4,128,800]{1,2,0:T(8,128)(2,1)}, u32[]{:S(2)}) copy-start(bf16[4,128,800]{1,2,0:T(8,128)(2,1)} %param.18) | copy-start | bytes 2457604
  7.2 104.7 %all-gather.2.cloned.1.call-start = ((), (), s32[]{:S(2)}) async-start(), calls=%async_computation.3 | async-start | bytes 13926400 | tf_op jit(solution)/shard_map/all_gather | solution.py:70
  10.9 257.2 %all-to-all-start = ((s32[16,1,2]{2,1,0:T(1,128)}), s32[16,1,2]{2,1,0:T(1,128)S(1)}, u32[]{:S(2)}, u32[]{:S(2)}) async-start(s32[16,1,2]{2,1,0:T(1,128)} %bitcast.13), calls=%async_computation | async-start | bytes 16384 | tf_op jit(solution)/shard_map/all_to_all | solution.py:153
  18.5 194.7 %all-reduce.4.cloned.1.call-start = ((), (), s32[]{:S(2)}) async-start(), calls=%async_computation.2 | async-start | bytes 3670016 | tf_op jit(solution)/shard_map/psum | solution.py:79
  21.6 3.8 copy-start.12
  21.6 3.9 copy-start.15
  21.6 3.9 copy-start.16
  21.6 3.9 copy-start.9
  26.1 3.1 copy-start.10
  42.4 1.8 copy-start.1
  44.2 3.1 copy-start.11
  45.4 1.9 copy-start.6
  213.2 3.1 copy-start.2
  213.2 3.9 copy-start.17
  216.2 4.1 copy-start
  216.2 2.7 copy-start.7
  220.3 1.8 copy-start.8
  228.1 3.1 copy-start.2
  228.1 3.9 copy-start.17
  231.1 4.1 copy-start
  231.1 2.7 copy-start.7
  235.2 1.8 copy-start.8
  268.1 99.9 %all-to-all-start.1 = ((bf16[16,2,128,800]{2,3,1,0:T(8,128)(2,1)}), bf16[16,2,128,800]{2,3,1,0:T(8,128)(2,1)}, u32[]{:S(2)}, u32[]{:S(2)}) async-start(bf16[16,2,128,800]{2,3,1,0:T(8,128)(2,1)} %bitcast.86), calls=%async_computation.1 | async-start | bytes 13107200 | tf_op jit(solution)/shard_map/all_to_all | solution.py:152
  272.7 317.9 %all-reduce.8.cloned.1.call-start = ((), (), s32[]{:S(2)}) async-start(), calls=%async_computation.5 | async-start | bytes 6553600 | tf_op jit(solution)/shard_map/psum | solution.py:167
  283.7 1.1 copy-start.4
  283.7 422.9 %all-reduce.6.cloned.1.call-start = ((), (), s32[]{:S(2)}) async-start(), calls=%async_computation.4 | async-start | bytes 3276800 | tf_op jit(solution)/shard_map/psum | solution.py:38
  404.4 11.1 %copy-start.13 = (f32[512]{0:T(512)S(1)}, f32[512]{0:T(512)}, u32[]{:S(2)}) copy-start(f32[512]{0:T(512)} %param.17) | copy-start | bytes 6148
  714.9 3.1 copy-start.14
  714.9 3.7 copy-start.5
Sparse Core Ops, SparseCore 0:
  10.4 101.3 all-gather.1
  115.2 97.9 all-reduce.3
  283.9 306.6 all-reduce.7
  592.9 113.6 all-reduce.5
where the time goes:
time: 730 us; the launch traced here: 729 us
  waiting for transfers between devices  508 us (70%)
  local copies, waits for them, and re-layouts  111 us (15%)
  other arithmetic  52.5 us (7%)
  matrix products  29.1 us (4%)
  between operations  14.8 us (2%)
  starting transfers between devices  12.4 us (2%)
    psum x1, waiting for transfers between devices, per_device(): neg_all = lax.psum(neg_part, ('head', 'tail'))  171 us
    psum x1, waiting for transfers between devices, head_sum(): return lax.psum(tail_grad, 'head')  116 us
    psum x1, waiting for transfers between devices, per_device(): lax.psum(own_negs.astype(jnp.float32).astype(jnp.bfloat16), 'tail')  81.2 us
    all_to_all x1, waiting for transfers between devices, per_device(): lax.all_to_all(outgoing, 'tail', split_axis=0, concat_axis=0, tiled=True)  76.1 us
    all_gather x1, waiting for transfers between devices, per_device(): partition = lax.all_gather(tail_emb, 'tail', axis=0, tiled=True)  63.1 us
  transfers between devices with their start and end apart: 6, of which 5 were waited for; matrix products, arithmetic and copies ran while one was open for 23% of the time, Pallas kernels for 0%

commit v1 on v0

v1 whole, which is shorter than its diff:
```python
import jax
import jax.numpy as jnp
from jax import lax
from jax.experimental import pallas as pl
from jax.experimental.pallas import tpu as pltpu
from jax.sharding import PartitionSpec as P

LEARN_RATE = 0.3
MESH = pl.DeviceIdType.MESH
F32 = jnp.float32
BF16 = jnp.bfloat16
SIDE = 4
DEPTH = 8
HEAD = 16
TAIL = 16


def greet(targets):
    barrier = pltpu.get_barrier_semaphore()
    for target in targets:
        pl.semaphore_signal(barrier, inc=1, device_id=target, device_id_type=MESH)
    pl.semaphore_wait(barrier, len(targets))


def table_gather(own, table, send1, recv1, send2, recv2, send3, recv3, local):
    head, tail = lax.axis_index("head"), lax.axis_index("tail")
    core, col, row = lax.rem(head, 2), lax.rem(tail, SIDE), lax.div(tail, SIDE)
    sibling = (head + 1 - 2 * core, tail)
    half = own.shape[1] // 2
    everything = (0, own.shape[1])
    first, second = (0, half), (half, half)

    def place(which, along, across):
        dx, dy = (along, across) if which == 0 else (across, along)
        return lax.rem(row + dy + SIDE, SIDE) * SIDE + lax.rem(col + dx + SIDE, SIDE)

    greet(
        [sibling]
        + [(head, place(0, 1, 0)), (head, place(0, -1, 0))]
        + [(head, place(1, 1, 0)), (head, place(1, -1, 0))]
    )

    def copy(which, origin, part, sems, spot, target):
        block = 2 * core + which
        start, size = part
        here = table.at[place(which, *origin), block, pl.ds(start, size)]
        source = own.at[block, pl.ds(start, size)] if origin == (0, 0) else here
        return pltpu.make_async_remote_copy(
            src_ref=source,
            dst_ref=here,
            send_sem=sems[0].at[which, spot],
            recv_sem=sems[1].at[which, spot],
            device_id=target,
            device_id_type=MESH,
        )

    def landing(which, origin, part, sems, spot):
        block = 2 * core + which
        start, size = part
        here = table.at[place(which, *origin), block, pl.ds(start, size)]
        return pltpu.make_async_remote_copy(
            src_ref=here,
            dst_ref=here,
            send_sem=sems[0].at[which, spot],
            recv_sem=sems[1].at[which, spot],
            device_id=sibling,
            device_id_type=MESH,
        )

    stage1, stage2, stage3 = (send1, recv1), (send2, recv2), (send3, recv3)
    sent = []

    def send(*description):
        transfer = copy(*description)
        transfer.start()
        sent.append(transfer)

    def spread(which, origin):
        spot = (origin[0] % SIDE) * 4
        send(which, origin, everything, stage2, spot, (head, place(which, 0, 1)))
        send(which, origin, everything, stage2, spot + 1, (head, place(which, 0, -1)))

    def share(which, origin):
        spot = (origin[0] % SIDE) * 4 + origin[1] % SIDE
        send(which, origin, everything, stage3, spot, sibling)

    for which in (0, 1):
        send(which, (0, 0), everything, stage1, 0, (head, place(which, 1, 0)))
        send(which, (0, 0), everything, stage1, 1, (head, place(which, -1, 0)))
    keep = pltpu.make_async_copy(own, table.at[tail], local)
    keep.start()
    for which in (0, 1):
        spread(which, (0, 0))
    for which in (0, 1):
        landing(which, (-1, 0), everything, stage1, 0).wait_recv()
        send(which, (-1, 0), first, stage1, 2, (head, place(which, 1, 0)))
        spread(which, (-1, 0))
        share(which, (-1, 0))
        landing(which, (1, 0), everything, stage1, 1).wait_recv()
        send(which, (1, 0), second, stage1, 3, (head, place(which, -1, 0)))
        spread(which, (1, 0))
        share(which, (1, 0))
    for which in (0, 1):
        landing(which, (2, 0), first, stage1, 2).wait_recv()
        landing(which, (2, 0), second, stage1, 3).wait_recv()
        spread(which, (2, 0))
        share(which, (2, 0))
    for along in (0, -1, 1, 2):
        spot = (along % SIDE) * 4
        for which in (0, 1):
            landing(which, (along, -1), everything, stage2, spot).wait_recv()
            send(which, (along, -1), first, stage2, spot + 2, (head, place(which, 0, 1)))
            share(which, (along, -1))
            landing(which, (along, 1), everything, stage2, spot + 1).wait_recv()
            send(which, (along, 1), second, stage2, spot + 3, (head, place(which, 0, -1)))
            share(which, (along, 1))
    for along in (0, -1, 1, 2):
        spot = (along % SIDE) * 4
        for which in (0, 1):
            landing(which, (along, 2), first, stage2, spot + 2).wait_recv()
            landing(which, (along, 2), second, stage2, spot + 3).wait_recv()
            share(which, (along, 2))
    for which in (0, 1):
        for along in range(SIDE):
            for across in range(SIDE):
                if (along, across) != (0, 0):
                    block = 2 * (1 - core) + which
                    here = table.at[place(which, along, across), block]
                    pltpu.make_async_remote_copy(
                        src_ref=here,
                        dst_ref=here,
                        send_sem=send3.at[which, along * 4 + across],
                        recv_sem=recv3.at[which, along * 4 + across],
                        device_id=sibling,
                        device_id_type=MESH,
                    ).wait_recv()
    keep.wait()
    for transfer in sent:
        transfer.wait_send()


def gather_table(tail_emb):
    shape = (TAIL,) + tail_emb.shape
    sems = pltpu.SemaphoreType.DMA
    return pl.pallas_call(
        table_gather,
        out_shape=jax.ShapeDtypeStruct(shape, tail_emb.dtype),
        in_specs=[pl.BlockSpec(memory_space=pl.ANY)],
        out_specs=pl.BlockSpec(memory_space=pl.ANY),
        scratch_shapes=[
            sems((2, 4)),
            sems((2, 4)),
            sems((2, 16)),
            sems((2, 16)),
            sems((2, 16)),
            sems((2, 16)),
            sems(()),
        ],
        compiler_params=pltpu.CompilerParams(collective_id=0, has_side_effects=True),
    )(tail_emb)


TN = (((0,), (0,)), ((), ()))
NT = (((1,), (1,)), ((), ()))


def mm(left, right, dims=(((1,), (0,)), ((), ()))):
    return lax.dot_general(left, right, dims, preferred_element_type=F32)


def one_hot(count, index_row):
    spots = lax.broadcasted_iota(jnp.int32, (count, index_row.shape[1]), 0)
    return jnp.where(spots == index_row, 1.0, 0.0).astype(BF16)


def edge_work(
    block_ids,
    neg_ids,
    live_count,
    table,
    head_emb,
    head_state,
    relation_emb,
    head_rows,
    relations,
    offsets,
    head_new,
    state_new,
    block_out,
    neg_out,
    chosen,
    negs,
    head_t,
    rel_t,
    neg_t,
    query_all,
    prob_all,
    grad_hi,
    grad_lo,
    sems,
):
    blocks, edges = head_rows.shape
    rows, width = head_emb.shape
    half = width // 2
    span = chosen.shape[1]
    neg_count = negs.shape[0]

    fetches = []
    for k in range(neg_count):
        fetches.append(pltpu.make_async_copy(table.at[neg_ids[k]], negs.at[k], sems.at[k]))
    for b in range(blocks):
        fetches.append(
            pltpu.make_async_copy(table.at[block_ids[b]], chosen.at[b], sems.at[neg_count + b])
        )
    for fetch in fetches:
        fetch.start()
    head_t[...] = head_emb[...].T
    rel_t[...] = relation_emb[...].T
    for fetch in fetches:
        fetch.wait()
    for k in range(neg_count):
        neg_t[:, k * span : (k + 1) * span] = negs[k].T

    def one_block(b, carry):
        lanes = pl.ds(pl.multiple_of(b * edges, edges), edges)
        live = jnp.where(b < live_count[0], 1.0, 0.0).astype(F32)
        pick = one_hot(span, offsets[pl.ds(b, 1), :])
        head_vec = mm(head_t[...], one_hot(rows, head_rows[pl.ds(b, 1), :]))
        rel_vec = mm(rel_t[...], one_hot(rel_t.shape[1], relations[pl.ds(b, 1), :]))
        tail_vec = mm(chosen[b], pick, TN)
        hr, hi = head_vec[:half], head_vec[half:]
        rr, ri = rel_vec[:half], rel_vec[half:]
        query = jnp.concatenate([hr * rr - hi * ri, hr * ri + hi * rr], axis=0).astype(BF16)
        query_all[:, lanes] = query
        query = query.astype(F32)
        positive = jnp.sum(query * tail_vec, axis=0, keepdims=True)
        score = mm(negs[...].reshape(neg_count * span, width), query_all[:, lanes])
        largest = jnp.maximum(positive, jnp.max(score, axis=0, keepdims=True))
        pos_exp = jnp.exp(positive - largest)
        neg_exp = jnp.exp(score - largest)
        denominator = pos_exp + jnp.sum(neg_exp, axis=0, keepdims=True)
        pos_grad = (pos_exp / denominator - 1.0) * live
        prob_all[:, lanes] = (neg_exp * (live / denominator)).astype(BF16)
        query_grad = pos_grad * tail_vec + mm(neg_t[...], prob_all[:, lanes])
        part = pos_grad * query
        part_a = part.astype(BF16)
        rest = part - part_a.astype(F32)
        part_b = rest.astype(BF16)
        part_c = (rest - part_b.astype(F32)).astype(BF16)
        block_grad = mm(pick, part_a, NT) + (mm(pick, part_b, NT) + mm(pick, part_c, NT))
        for i in range(HEAD):
            block_out[i, b] = block_grad[i * 8 : (i + 1) * 8].astype(BF16)
        qr, qi = query_grad[:half], query_grad[half:]
        change = jnp.concatenate([qr * rr + qi * ri, qi * rr - qr * ri], axis=0)
        change_hi = change.astype(BF16)
        grad_hi[:, lanes] = change_hi
        grad_lo[:, lanes] = (change - change_hi.astype(F32)).astype(BF16)
        return carry

    lax.fori_loop(0, blocks, one_block, 0)

    def neg_rows(k, carry):
        span_rows = pl.ds(pl.multiple_of(k * 256, 256), 256)
        neg_out[span_rows, :] = mm(prob_all[span_rows, :], query_all[...], NT)
        return carry

    lax.fori_loop(0, neg_count * span // 256, neg_rows, 0)

    diagonal = lax.broadcasted_iota(jnp.int32, (128, 128), 0) == lax.broadcasted_iota(
        jnp.int32, (128, 128), 1
    )
    for part in range(rows // 128):
        span_rows = pl.ds(part * 128, 128)
        spots = lax.broadcasted_iota(jnp.int32, (128, edges), 0) + part * 128
        gradient = jnp.zeros((128, width), F32)
        for b in range(blocks):
            hot = jnp.where(spots == head_rows[b : b + 1, :], 1.0, 0.0).astype(BF16)
            lanes = pl.ds(b * edges, edges)
            gradient += mm(hot, grad_hi[:, lanes], NT) + mm(hot, grad_lo[:, lanes], NT)
        state_row = head_state[:, span_rows]
        state_column = jnp.sum(jnp.where(diagonal, state_row, 0.0), axis=1, keepdims=True)
        state_next = state_column + jnp.sum(gradient * gradient, axis=1, keepdims=True) / width
        head_new[span_rows, :] = (
            head_emb[span_rows, :].astype(F32) - gradient * (LEARN_RATE / jnp.sqrt(state_next))
        ).astype(BF16)
        state_new[:, span_rows] = jnp.sum(
            jnp.where(diagonal, state_next, 0.0), axis=0, keepdims=True
        )


def run_edges(
    block_ids,
    neg_ids,
    live_count,
    table,
    head_emb,
    head_state,
    relation_emb,
    head_rows,
    relations,
    offsets,
):
    blocks, edges = head_rows.shape
    rows, width = head_emb.shape
    span = table.shape[1]
    negs = neg_ids.shape[0]
    total = blocks * edges
    smem = pl.BlockSpec(memory_space=pltpu.SMEM)
    vmem = pl.BlockSpec(memory_space=pltpu.VMEM)
    rels = relation_emb.shape[0]
    return pl.pallas_call(
        edge_work,
        out_shape=(
            jax.ShapeDtypeStruct((rows, width), BF16),
            jax.ShapeDtypeStruct((1, rows), F32),
            jax.ShapeDtypeStruct((HEAD, blocks, span // HEAD, width), BF16),
            jax.ShapeDtypeStruct((negs * span, width), F32),
        ),
        in_specs=[smem, smem, smem, pl.BlockSpec(memory_space=pl.ANY)] + [vmem] * 6,
        out_specs=(vmem, vmem, vmem, vmem),
        scratch_shapes=[
            pltpu.VMEM((blocks, span, width), BF16),
            pltpu.VMEM((negs, span, width), BF16),
            pltpu.VMEM((width, rows), BF16),
            pltpu.VMEM((width, rels), BF16),
            pltpu.VMEM((width, negs * span), BF16),
            pltpu.VMEM((width, total), BF16),
            pltpu.VMEM((negs * span, total), BF16),
            pltpu.VMEM((width, total), BF16),
            pltpu.VMEM((width, total), BF16),
            pltpu.SemaphoreType.DMA((blocks + negs,)),
        ],
        compiler_params=pltpu.CompilerParams(vmem_limit_bytes=56 << 20),
    )(
        block_ids,
        neg_ids,
        live_count,
        table,
        head_emb,
        head_state,
        relation_emb,
        head_rows,
        relations,
        offsets,
    )


def exchange(
    neg_ids,
    block_part,
    places,
    neg_part,
    own_rows,
    own_state,
    out,
    state_out,
    slots,
    seats,
    theirs,
    mine,
    planes,
    deep,
    deep_in,
    neg_total,
    slot_rows,
    dense,
    dense_in,
    rows_now,
    update,
    state_next,
    sem_bs,
    sem_br,
    sem_is,
    sem_ir,
    sem_cs,
    sem_cr,
    sem_cl,
    sem_ps,
    sem_pr,
    sem_zs,
    sem_zr,
    sem_ds,
    sem_dr,
    sem_ns,
    sem_nr,
    sem_us,
    sem_ur,
    sem_ws,
    sem_wr,
    sem_fs,
    sem_fr,
    sem_gs,
    sem_gr,
    sem_local,
):
    head, tail = lax.axis_index("head"), lax.axis_index("tail")
    core, depth = lax.rem(head, 2), lax.div(head, 2)
    other = head + 1 - 2 * core
    owned = own_rows.shape[0]
    quarter = DEPTH // 2
    width = own_rows.shape[-1]

    def around(index, step, count):
        return lax.rem(index + step, count)

    def remote(source, target, send_sem, recv_sem, device):
        return pltpu.make_async_remote_copy(
            src_ref=source,
            dst_ref=target,
            send_sem=send_sem,
            recv_sem=recv_sem,
            device_id=device,
            device_id_type=MESH,
        )

    barrier = pltpu.get_barrier_semaphore()

    @pl.loop(1, HEAD)
    def _(step):
        pl.semaphore_signal(
            barrier, inc=1, device_id=(around(head, step, HEAD), tail), device_id_type=MESH
        )
        pl.semaphore_signal(
            barrier, inc=1, device_id=(head, around(tail, step, TAIL)), device_id_type=MESH
        )

    pl.semaphore_wait(barrier, HEAD + TAIL - 2)

    def chunk(peer, side):
        return neg_part.at[lax.div(peer, 2), pl.ds(lax.rem(peer, 2) * quarter, quarter), side]

    def pair_copy(step):
        peer = around(tail, step, TAIL)
        return remote(
            chunk(peer, 1 - core), theirs.at[peer], sem_cs.at[step], sem_cr.at[step], (other, tail)
        )

    def pair_local(step):
        peer = around(tail, step, TAIL)
        return pltpu.make_async_copy(chunk(peer, core), mine.at[peer], sem_cl.at[step])

    @pl.loop(0, TAIL)
    def _(step):
        pair_copy(step).start()
        pair_local(step).start()

    def block_copy(step):
        return remote(
            block_part.at[around(head, step, HEAD)],
            slots.at[head],
            sem_bs.at[step],
            sem_br.at[step],
            (around(head, step, HEAD), tail),
        )

    def seat_copy(step):
        return remote(
            places,
            seats.at[head],
            sem_is.at[step],
            sem_ir.at[step],
            (around(head, step, HEAD), tail),
        )

    @pl.loop(1, HEAD)
    def _(step):
        block_copy(step).start()
        seat_copy(step).start()

    keep_block = pltpu.make_async_copy(block_part.at[head], slots.at[head], sem_local.at[0])
    keep_block.start()
    keep_rows = pltpu.make_async_copy(own_rows.at[:, head], rows_now, sem_local.at[1])
    keep_rows.start()
    seats[head] = places[...]

    def plane_copy(step):
        peer = around(tail, step, TAIL)
        return remote(
            mine.at[peer], planes.at[tail], sem_ps.at[step], sem_pr.at[step], (head, peer)
        )

    @pl.loop(1, TAIL)
    def _(step):
        peer = around(tail, step, TAIL)
        pair_copy(step).wait_recv()
        pair_local(step).wait()
        mine[peer] = mine[peer] + theirs[peer]
        plane_copy(step).start()

    pair_copy(0).wait_recv()
    pair_local(0).wait()
    planes[tail] = mine[tail] + theirs[tail]

    @pl.loop(1, HEAD)
    def _(step):
        block_copy(step).wait_recv()
        seat_copy(step).wait_recv()

    keep_block.wait()

    @pl.loop(0, HEAD)
    def _(source):
        for b in range(owned):
            slot_rows[pl.ds(pl.multiple_of(source * owned * 8 + b * 8, 8), 8), :] = slots[
                source, b
            ].astype(F32)

    seat_row = jnp.concatenate(
        [
            seats[4 * q, 0:1] + seats[4 * q + 1, 0:1] + seats[4 * q + 2, 0:1] + seats[4 * q + 3, 0:1]
            for q in range(HEAD // 4)
        ],
        axis=1,
    )
    hot = one_hot(TAIL * owned * 8, seat_row)
    dense[...] = mm(hot, slot_rows[...].astype(BF16)).reshape(dense.shape)

    @pl.loop(1, TAIL)
    def _(step):
        plane_copy(step).wait_recv()

    deep[...] = jnp.zeros_like(deep)

    @pl.loop(0, TAIL)
    def _(source):
        deep[...] += planes[source]

    zone = lax.rem(tail, 2)
    takes = lax.div(depth, quarter) == zone

    def deep_copy(step):
        level = zone * quarter + step
        return remote(
            deep.at[step],
            deep_in.at[depth],
            sem_zs.at[step],
            sem_zr.at[depth],
            (level * 2 + core, tail),
        )

    def deep_landing(source):
        return remote(
            deep.at[0], deep_in.at[source], sem_zs.at[0], sem_zr.at[source], (other, tail)
        )

    @pl.loop(0, quarter)
    def _(step):
        @pl.when(zone * quarter + step != depth)
        def _():
            deep_copy(step).start()

    @pl.when(takes)
    def _():
        deep_in[depth] = deep[depth - zone * quarter]

    def dense_copy(step):
        peer = around(tail, step, TAIL)
        return remote(
            dense.at[peer], dense_in.at[tail], sem_ds.at[step], sem_dr.at[step], (head, peer)
        )

    @pl.loop(1, TAIL)
    def _(step):
        dense_copy(step).start()

    dense_in[tail] = dense[tail]
    mine_k = lax.div(tail, 2)

    def total_copy(step):
        return remote(
            neg_total.at[mine_k],
            neg_total.at[mine_k],
            sem_ns.at[step],
            sem_nr.at[mine_k],
            (head, around(tail, step, TAIL)),
        )

    def total_landing(k):
        return remote(
            neg_total.at[k], neg_total.at[k], sem_ns.at[1], sem_nr.at[k], (other, tail)
        )

    @pl.when(takes)
    def _():
        @pl.loop(0, DEPTH)
        def _(source):
            @pl.when(source != depth)
            def _():
                deep_landing(source).wait_recv()

        total = deep_in[0]
        for source in range(1, DEPTH):
            total = total + deep_in[source]
        neg_total[mine_k] = total

        @pl.loop(1, TAIL)
        def _(step):
            total_copy(step).start()

    @pl.loop(1, TAIL)
    def _(step):
        dense_copy(step).wait_recv()

    @pl.loop(0, neg_total.shape[0])
    def _(k):
        @pl.when(2 * k + lax.div(depth, quarter) != tail)
        def _():
            total_landing(k).wait_recv()

    keep_rows.wait()
    for b in range(owned):
        gradient = dense_in[0, b * 8 : (b + 1) * 8]
        for source in range(1, TAIL):
            gradient = gradient + dense_in[source, b * 8 : (b + 1) * 8]
        for k in range(neg_total.shape[0]):
            weight = jnp.where(neg_ids[k] == tail * owned + b, 1.0, 0.0).astype(F32)
            gradient = gradient + weight * neg_total[k]
        fresh = (
            own_state[b * 8 : (b + 1) * 8, 0:1]
            + jnp.sum(gradient * gradient, axis=1, keepdims=True) / width
        )
        state_next[b * 8 : (b + 1) * 8, :] = jnp.broadcast_to(fresh, (8, state_next.shape[1]))
        update[b] = (
            rows_now[b].astype(F32) - gradient * (LEARN_RATE / jnp.sqrt(fresh))
        ).astype(BF16)

    def rows_copy(step):
        return remote(
            update,
            out.at[:, head],
            sem_us.at[step],
            sem_ur.at[step],
            (around(depth, step, DEPTH) * 2 + core, tail),
        )

    def state_copy(step):
        return remote(
            state_next,
            state_out.at[head],
            sem_ws.at[step],
            sem_wr.at[step],
            (around(depth, step, DEPTH) * 2 + core, tail),
        )

    def source_of(step):
        return around(depth, DEPTH - step, DEPTH) * 2 + core

    @pl.loop(1, DEPTH)
    def _(step):
        rows_copy(step).start()
        state_copy(step).start()

    out_own = pltpu.make_async_copy(update, out.at[:, head], sem_local.at[2])
    out_own.start()
    state_own = pltpu.make_async_copy(state_next, state_out.at[head], sem_local.at[3])
    state_own.start()
    first_rows = remote(update, out.at[:, head], sem_fs.at[0], sem_fr.at[0], (other, tail))
    first_state = remote(state_next, state_out.at[head], sem_gs.at[0], sem_gr.at[0], (other, tail))
    first_rows.start()
    first_state.start()

    def pass_rows(step):
        place = source_of(step)
        return remote(
            out.at[:, place], out.at[:, place], sem_fs.at[step], sem_fr.at[step], (other, tail)
        )

    def pass_state(step):
        place = source_of(step)
        return remote(
            state_out.at[place],
            state_out.at[place],
            sem_gs.at[step],
            sem_gr.at[step],
            (other, tail),
        )

    @pl.loop(1, DEPTH)
    def _(step):
        rows_copy(step).wait_recv()
        pass_rows(step).start()
        state_copy(step).wait_recv()
        pass_state(step).start()

    out_own.wait()
    state_own.wait()
    first_rows.wait()
    first_state.wait()

    @pl.loop(1, DEPTH)
    def _(step):
        pass_rows(step).wait()
        pass_state(step).wait()
        rows_copy(step).wait_send()
        state_copy(step).wait_send()

    pair_copy(0).wait_send()

    @pl.loop(1, TAIL)
    def _(step):
        block_copy(step).wait_send()
        seat_copy(step).wait_send()
        pair_copy(step).wait_send()
        plane_copy(step).wait_send()
        dense_copy(step).wait_send()

    @pl.loop(0, quarter)
    def _(step):
        @pl.when(zone * quarter + step != depth)
        def _():
            deep_copy(step).wait_send()

    @pl.when(takes)
    def _():
        @pl.loop(1, TAIL)
        def _(step):
            total_copy(step).wait_send()


def run_exchange(neg_ids, block_part, places, neg_part, own_rows, own_state):
    owned, _, group, width = own_rows.shape
    negs = neg_ids.shape[0]
    quarter = DEPTH // 2
    sems = pltpu.SemaphoreType.DMA
    anywhere = pl.BlockSpec(memory_space=pl.ANY)
    vmem = pl.BlockSpec(memory_space=pltpu.VMEM)
    rows = owned * group
    return pl.pallas_call(
        exchange,
        out_shape=(
            jax.ShapeDtypeStruct(own_rows.shape, BF16),
            jax.ShapeDtypeStruct((HEAD, rows, 128), F32),
        ),
        in_specs=[
            pl.BlockSpec(memory_space=pltpu.SMEM),
            anywhere,
            vmem,
            anywhere,
            anywhere,
            vmem,
        ],
        out_specs=(anywhere, anywhere),
        scratch_shapes=[
            pltpu.VMEM((HEAD, owned, group, width), BF16),
            pltpu.VMEM((HEAD, 8, 128), jnp.int32),
            pltpu.VMEM((TAIL, quarter, group, width), F32),
            pltpu.VMEM((TAIL, quarter, group, width), F32),
            pltpu.VMEM((TAIL, quarter, group, width), F32),
            pltpu.VMEM((quarter, group, width), F32),
            pltpu.VMEM((DEPTH, group, width), F32),
            pltpu.VMEM((negs, group, width), F32),
            pltpu.VMEM((HEAD * rows, width), F32),
            pltpu.VMEM((TAIL, rows, width), F32),
            pltpu.VMEM((TAIL, rows, width), F32),
            pltpu.VMEM((owned, group, width), BF16),
            pltpu.VMEM((owned, group, width), BF16),
            pltpu.VMEM((rows, 128), F32),
            sems((HEAD,)),
            sems((HEAD,)),
            sems((HEAD,)),
            sems((HEAD,)),
            sems((TAIL,)),
            sems((TAIL,)),
            sems((TAIL,)),
            sems((TAIL,)),
            sems((TAIL,)),
            sems((quarter,)),
            sems((DEPTH,)),
            sems((TAIL,)),
            sems((TAIL,)),
            sems((TAIL,)),
            sems((negs,)),
            sems((DEPTH,)),
            sems((DEPTH,)),
            sems((DEPTH,)),
            sems((DEPTH,)),
            sems((DEPTH,)),
            sems((DEPTH,)),
            sems((DEPTH,)),
            sems((DEPTH,)),
            sems((4,)),
        ],
        compiler_params=pltpu.CompilerParams(
            collective_id=1, has_side_effects=True, vmem_limit_bytes=40 << 20
        ),
    )(neg_ids, block_part, places, neg_part, own_rows, own_state)


def per_device(
    head_emb,
    head_state,
    tail_emb,
    tail_state,
    relation_emb,
    head_rows,
    relations,
    tail_offsets,
    tail_owner,
    tail_local,
    block_count,
    neg_blocks,
):
    owned, span, width = tail_emb.shape
    blocks = tail_local.shape[0]
    head = lax.axis_index("head")
    group = span // HEAD
    block_ids = tail_owner[:, 0] * owned + tail_local
    lane = jnp.arange(128, dtype=jnp.int32)
    base = (head % 4) * blocks * group
    inside = (lane >= base) & (lane < base + blocks * group)
    spot = jnp.clip(lane - base, 0, blocks * group - 1)
    hits = (spot[:, None] // group) == jnp.arange(blocks, dtype=jnp.int32)[None, :]
    block_of = jnp.sum(jnp.where(hits, block_ids[None, :], 0), axis=1)
    places = jnp.where(inside, block_of * group + spot % group, 0)
    places = jnp.broadcast_to(places[None, :], (8, 128)).astype(jnp.int32)
    own_state = lax.dynamic_index_in_dim(
        tail_state.reshape(owned, HEAD, group), head, axis=1, keepdims=False
    )
    own_state = jnp.broadcast_to(own_state.reshape(owned * group, 1), (owned * group, 128))

    table = gather_table(tail_emb)
    head_new, head_state_new, block_part, neg_part = run_edges(
        block_ids,
        neg_blocks,
        block_count,
        table.reshape(TAIL * owned, span, width),
        head_emb,
        head_state[None, :],
        relation_emb,
        head_rows,
        relations,
        tail_offsets,
    )
    tail_new, tail_state_new = run_exchange(
        neg_blocks,
        block_part,
        places,
        neg_part.reshape(neg_blocks.shape[0], DEPTH, 2, group, width),
        tail_emb.reshape(owned, HEAD, group, width),
        own_state,
    )
    tail_state_new = tail_state_new[:, :, 0].reshape(HEAD, owned, group)
    tail_state_new = tail_state_new.transpose(1, 0, 2).reshape(owned, span)
    return (head_new, head_state_new[0], tail_new.reshape(owned, span, width), tail_state_new)


def solution(mesh):
    placed = (
        P(("head", "tail"), None),
        P(("head", "tail")),
        P("tail", None, None),
        P("tail", None),
        P(),
        P(("head", "tail"), None),
        P(("head", "tail"), None),
        P(("head", "tail"), None),
        P(("head", "tail"), None),
        P(("head", "tail")),
        P(("head", "tail")),
        P(),
    )
    return jax.shard_map(
        per_device,
        mesh=mesh,
        in_specs=placed,
        out_specs=(
            P(("head", "tail"), None),
            P(("head", "tail")),
            P("tail", None, None),
            P("tail", None),
        ),
        check_vma=False,
    )
```

time: 730 us -> 185 us (0.25)
  waiting for transfers between devices: 508 us -> 0 us
  Pallas kernels: 0 us -> 168 us
  local copies, waits for them, and re-layouts: 111 us -> 13.9 us
  other arithmetic: 52.5 us -> 1.3 us
  matrix products: 29.1 us -> 0 us
  between operations: 14.8 us -> 1.36 us
  starting transfers between devices: 12.4 us -> 0 us
    psum x3 -> x0, waiting for transfers between devices: 368 us -> none  [the longest x1 171 us: per_device(): neg_all = lax.psum(neg_part, ('head', 'tail'))]
    pallas_call x0 -> x3, Pallas kernels: none -> 168 us  [the longest x1 90.2 us: run_exchange(): pl.pallas_call(exchange, out_shape=(jax.ShapeDtypeStruct(own_rows.shape,...]
    all_to_all x2 -> x0, waiting for transfers between devices: 76.1 us -> none  [the longest x1 76.1 us: per_device(): lax.all_to_all(outgoing, 'tail', split_axis=0, concat_axis=0, tiled=True)]
    all_gather x1 -> x0, waiting for transfers between devices: 63.1 us -> none  [per_device(): partition = lax.all_gather(tail_emb, 'tail', axis=0, tiled=True)]
    dot_general x8 -> x0, matrix products: 29.1 us -> none  [the longest x2 9.9 us: score_group(): lax.dot_general(neg_grad, query_rows, (((0,), (0,)), ((), ())), preferred...]
    reshape x4 -> x2, local copies, waits for them, and re-layouts: 25.6 us -> 0.76 us  [the longest x1 0.68 us: per_device(): tail_state_new = tail_state_new.transpose(1, 0, 2).reshape(owned, span)]
    gather x6 -> x0, local copies, waits for them, and re-layouts: 23.4 us -> none  [the longest x2 6.69 us: per_device(): chosen = jnp.take(partition, global_block, axis=0)]
    scatter-add x2 -> x0, other arithmetic: 21.7 us -> none  [the longest x1 10.9 us: per_device(): head_grad = jnp.zeros(head_emb.shape, jnp.float32).at[flat_rows].add(conj...]
  transfers between devices with their start and end apart: 6 -> 0, of which waited for: 5 -> 0; matrix products, arithmetic and copies ran while one was open for 23% -> 0% of each run, Pallas kernels for 0% -> 0%
where the time goes in v1:
time: 185 us; the launch traced here: 184 us
  Pallas kernels  168 us (91%)
  local copies, waits for them, and re-layouts  13.9 us (8%)
    pallas_call x1, Pallas kernels, run_exchange(): pl.pallas_call(exchange, out_shape=(jax.ShapeDtypeStruct(own_rows.shape,...  90.2 us
    pallas_call x1, Pallas kernels, gather_table(): pl.pallas_call(table_gather, out_shape=jax.ShapeDtypeStruct(shape, tail_e...  48.8 us
    pallas_call x1, Pallas kernels, run_edges(): pl.pallas_call(edge_work, out_shape=(jax.ShapeDtypeStruct((rows, width),...  29 us
    unnamed x21, local copies, waits for them, and re-layouts  12.6 us

profile of v1, /device:TPU:1, one launch (start us, length us, event | category | flops | bytes accessed | tf_op | source)
XLA Modules:
  0.0 184.5 jit_solution(14242403994502196723)
XLA Ops:
  0.6 1.2 bitcast_add_fusion.block_ids
  2.5 2.2 %copy.32.own = bf16[4,128,800]{2,1,0:T(8,128)(2,1)} copy(bf16[4,128,800]{1,2,0:T(8,128)(2,1)} %param.14) | data formatting | bytes 1638400 | tf_op args[2]
  4.7 0.0 copy-start.5
  4.7 0.0 copy-start.4
  4.7 48.8 %shard_map.147 = bf16[16,4,128,800]{3,2,1,0:T(8,128)(2,1)} custom-call(bf16[4,128,800]{2,1,0:T(8,128)(2,1)} %copy.32.own), custom_call_target="tpu_custom_call" | custom-call | tf_op jit(solution)/shard_map/pallas_call | solution.py:145
  53.5 0.0 copy-done.5
  53.5 1.3 copy.33.head_emb
  54.8 0.0 copy-done.4
  54.8 2.4 %copy.34.relation_emb = bf16[1024,800]{1,0:T(8,128)(2,1)} copy(bf16[1024,800]{0,1:T(8,128)(2,1)S(1)} %copy-done.4) | data formatting | bytes 3276800 | tf_op args[4]
  57.2 0.0 copy-start.7
  57.2 0.0 copy-start.6
  57.2 0.0 copy-start
  57.3 0.0 copy-start.3
  57.3 29.0 %shard_map.148 = (bf16[512,800]{1,0:T(8,128)(2,1)}, f32[1,512]{1,0:T(1,128)}, bf16[16,4,8,800]{3,2,1,0:T(8,128)(2,1)}, f32[1024,800]{1,0:T(8,128)}) custom-call(s32[4]{0:T(128)} %bitcast_add_fusion.block_ids, s32[8]{0:T(128)} %neg_ids.3, s32[1]{0:T(128)S(6)} %copy.40.live_count, bf16[64,128,800]{2,1,0:T(8,128)(2,1)} %bitcast.16, ...), custom_call_target="tpu_custom_call" | custom-call | tf_op jit(solution)/shard_map/pallas_call | solution.py:311
  86.2 2.2 %copy.38 = bf16[512,800]{0,1:T(8,128)(2,1)} copy(bf16[512,800]{1,0:T(8,128)(2,1)} %get-tuple-element.24) | data formatting | bytes 1638400
  88.4 0.0 copy-done.7
  88.4 0.1 select_reduce_fusion
  88.5 0.0 copy-done.6
  88.5 0.1 reshape.99
  88.6 0.1 broadcast_in_dim.37
  88.7 0.1 broadcast_in_dim.38.own_state
  88.8 0.0 copy-done
  88.8 0.0 copy-done.3
  88.8 0.0 copy-start.1
  88.8 2.0 %copy-done.1 = f32[1024,800]{1,0:T(8,128)S(1)} copy-done((f32[1024,800]{1,0:T(8,128)S(1)}, f32[1024,800]{1,0:T(8,128)}, u32[]{:S(2)}) %copy-start.1) | copy-done | bytes 3276824
  90.8 0.0 copy-start.2
  90.8 1.2 copy-done.2
  92.0 90.2 %shard_map.149 = (bf16[4,16,8,800]{3,2,1,0:T(8,128)(2,1)S(1)}, f32[16,32,128]{2,1,0:T(8,128)S(1)}) custom-call(s32[8]{0:T(128)S(1)} %copy-done.3, bf16[16,4,8,800]{3,2,1,0:T(8,128)(2,1)S(1)} %copy-done.2, s32[8,128]{1,0:T(8,128)S(1)} %broadcast_in_dim.36.places, f32[8,8,2,8,800]{4,3,2,1,0:T(8,128)S(1)} %bitcast.13, bf16[4,16,8,800]{3,2,1,0:T(8,128)(2,1)S(1)} %bitcast.12, ...), custom_call_target="tpu_custom_call" | custom-call | tf_op jit(solution)/shard_map/pallas_call | solution.py:728
  182.2 1.3 copy.39
  183.5 0.3 copy.36
  183.7 0.1 copy.37
  183.8 0.7 reshape.101
  (4 shorter events, 0.1 us)
Async XLA Ops:
  4.7 48.8 %copy-start.5 = (bf16[512,800]{0,1:T(8,128)(2,1)S(1)}, bf16[512,800]{0,1:T(8,128)(2,1)}, u32[]{:S(2)}) copy-start(bf16[512,800]{0,1:T(8,128)(2,1)} %param.12) | copy-start | bytes 2457604
  4.7 50.1 %copy-start.4 = (bf16[1024,800]{0,1:T(8,128)(2,1)S(1)}, bf16[1024,800]{0,1:T(8,128)(2,1)}, u32[]{:S(2)}) copy-start(bf16[1024,800]{0,1:T(8,128)(2,1)} %param.16) | copy-start | bytes 4915204
  57.2 31.1 %copy-start.7 = (s32[4]{0:T(128)S(1)}, s32[4]{0:T(128)}, u32[]{:S(2)}) copy-start(s32[4]{0:T(128)} %bitcast_add_fusion.block_ids) | copy-start | bytes 52
  57.2 31.3 %copy-start.6 = (f32[4,128]{1,0:T(4,128)S(1)}, f32[4,128]{1,0:T(4,128)}, u32[]{:S(2)}) copy-start(f32[4,128]{1,0:T(4,128)} %param.15) | copy-start | bytes 6148
  57.2 31.5 %copy-start = (bf16[4,128,800]{2,1,0:T(8,128)(2,1)S(1)}, bf16[4,128,800]{2,1,0:T(8,128)(2,1)}, u32[]{:S(2)}) copy-start(bf16[4,128,800]{2,1,0:T(8,128)(2,1)} %copy.32.own) | copy-start | bytes 2457604
  57.3 31.5 %copy-start.3 = (s32[8]{0:T(128)S(1)}, s32[8]{0:T(128)}, u32[]{:S(2)}) copy-start(s32[8]{0:T(128)} %neg_ids.3) | copy-start | bytes 100
  88.8 2.0 %copy-start.1 = (f32[1024,800]{1,0:T(8,128)S(1)}, f32[1024,800]{1,0:T(8,128)}, u32[]{:S(2)}) copy-start(f32[1024,800]{1,0:T(8,128)} %get-tuple-element.13) | copy-start | bytes 9830404
  90.8 1.2 copy-start.2

commit v2 on v1

v2 whole, which is shorter than its diff:
```python
import jax
import jax.numpy as jnp
from jax import lax
from jax.experimental import pallas as pl
from jax.experimental.pallas import tpu as pltpu
from jax.sharding import PartitionSpec as P

LEARN_RATE = 0.3
MESH = pl.DeviceIdType.MESH
F32 = jnp.float32
BF16 = jnp.bfloat16
SIDE = 4
DEPTH = 8
HEAD = 16
TAIL = 16
LANES = 896


def greet(targets):
    barrier = pltpu.get_barrier_semaphore()
    for target in targets:
        pl.semaphore_signal(barrier, inc=1, device_id=target, device_id_type=MESH)
    pl.semaphore_wait(barrier, len(targets))


TN = (((0,), (0,)), ((), ()))
NT = (((1,), (1,)), ((), ()))


def mm(left, right, dims=(((1,), (0,)), ((), ()))):
    return lax.dot_general(left, right, dims, preferred_element_type=F32)


def one_hot(count, index_row):
    spots = lax.broadcasted_iota(jnp.int32, (count, index_row.shape[1]), 0)
    return jnp.where(spots == index_row, 1.0, 0.0).astype(BF16)


def table_gather(
    own,
    head_hbm,
    rel_hbm,
    head_rows,
    relations,
    table,
    query_out,
    rel_out,
    head_t,
    rel_t,
    query,
    rel_vec,
    send1,
    recv1,
    send2,
    recv2,
    send3,
    recv3,
    local,
):
    head, tail = lax.axis_index("head"), lax.axis_index("tail")
    core, col, row = lax.rem(head, 2), lax.rem(tail, SIDE), lax.div(tail, SIDE)
    sibling = (head + 1 - 2 * core, tail)
    size = own.shape[1]
    everything = (0, size)
    first, second = (0, size // 2), (size // 2, size // 2)
    blocks = query.shape[0]

    loads = [
        pltpu.make_async_copy(head_hbm, head_t, local.at[0]),
        pltpu.make_async_copy(rel_hbm, rel_t, local.at[1]),
        pltpu.make_async_copy(own, table.at[tail], local.at[2]),
    ]
    for load in loads:
        load.start()

    def place(which, along, across):
        dx, dy = (along, across) if which == 0 else (across, along)
        return lax.rem(row + dy + SIDE, SIDE) * SIDE + lax.rem(col + dx + SIDE, SIDE)

    greet(
        [sibling]
        + [(head, place(0, 1, 0)), (head, place(0, -1, 0))]
        + [(head, place(1, 1, 0)), (head, place(1, -1, 0))]
    )

    def copy(which, origin, part, sems, spot, target):
        block = 2 * core + which
        start, count = part
        here = table.at[place(which, *origin), block, pl.ds(start, count)]
        source = own.at[block, pl.ds(start, count)] if origin == (0, 0) else here
        return pltpu.make_async_remote_copy(
            src_ref=source,
            dst_ref=here,
            send_sem=sems[0].at[which, spot],
            recv_sem=sems[1].at[which, spot],
            device_id=target,
            device_id_type=MESH,
        )

    def landing(which, origin, part, sems, spot, block=None):
        block = 2 * core + which if block is None else block
        start, count = part
        here = table.at[place(which, *origin), block, pl.ds(start, count)]
        return pltpu.make_async_remote_copy(
            src_ref=here,
            dst_ref=here,
            send_sem=sems[0].at[which, spot],
            recv_sem=sems[1].at[which, spot],
            device_id=sibling,
            device_id_type=MESH,
        )

    stage1, stage2, stage3 = (send1, recv1), (send2, recv2), (send3, recv3)
    sent = []

    def send(*description):
        transfer = copy(*description)
        transfer.start()
        sent.append(transfer)

    def spread(which, origin):
        spot = (origin[0] % SIDE) * 4
        send(which, origin, everything, stage2, spot, (head, place(which, 0, 1)))
        send(which, origin, everything, stage2, spot + 1, (head, place(which, 0, -1)))

    def share(which, origin):
        spot = (origin[0] % SIDE) * 4 + origin[1] % SIDE
        send(which, origin, everything, stage3, spot, sibling)

    stores = []

    def make_query(b):
        half = size // 2
        vec = mm(head_t[...], one_hot(head_t.shape[1], head_rows[b : b + 1, :]))
        rel = mm(rel_t[...], one_hot(rel_t.shape[1], relations[b : b + 1, :]))
        rel_vec[b] = rel.astype(BF16)
        query[b, :half] = (vec[:half] * rel[:half] - vec[half:] * rel[half:]).astype(BF16)
        query[b, half:] = (vec[:half] * rel[half:] + vec[half:] * rel[:half]).astype(BF16)
        for value, target, spot in ((query, query_out, 3), (rel_vec, rel_out, 3 + blocks)):
            store = pltpu.make_async_copy(value.at[b], target.at[b], local.at[spot + b])
            store.start()
            stores.append(store)

    for which in (0, 1):
        send(which, (0, 0), everything, stage1, 0, (head, place(which, 1, 0)))
        send(which, (0, 0), everything, stage1, 1, (head, place(which, -1, 0)))
    for which in (0, 1):
        spread(which, (0, 0))
    loads[0].wait()
    loads[1].wait()
    make_query(0)
    for which in (0, 1):
        landing(which, (-1, 0), everything, stage1, 0).wait_recv()
        send(which, (-1, 0), first, stage1, 2, (head, place(which, 1, 0)))
        spread(which, (-1, 0))
        share(which, (-1, 0))
        landing(which, (1, 0), everything, stage1, 1).wait_recv()
        send(which, (1, 0), second, stage1, 3, (head, place(which, -1, 0)))
        spread(which, (1, 0))
        share(which, (1, 0))
    for b in range(1, blocks - 1):
        make_query(b)
    for which in (0, 1):
        landing(which, (2, 0), first, stage1, 2).wait_recv()
        landing(which, (2, 0), second, stage1, 3).wait_recv()
        spread(which, (2, 0))
        share(which, (2, 0))
    for along in (0, -1, 1, 2):
        spot = (along % SIDE) * 4
        for which in (0, 1):
            landing(which, (along, -1), everything, stage2, spot).wait_recv()
            send(which, (along, -1), first, stage2, spot + 2, (head, place(which, 0, 1)))
            share(which, (along, -1))
            landing(which, (along, 1), everything, stage2, spot + 1).wait_recv()
            send(which, (along, 1), second, stage2, spot + 3, (head, place(which, 0, -1)))
            share(which, (along, 1))
        if along == 0:
            make_query(blocks - 1)
    for along in (0, -1, 1, 2):
        spot = (along % SIDE) * 4
        for which in (0, 1):
            landing(which, (along, 2), first, stage2, spot + 2).wait_recv()
            landing(which, (along, 2), second, stage2, spot + 3).wait_recv()
            share(which, (along, 2))
    for which in (0, 1):
        for along in range(SIDE):
            for across in range(SIDE):
                if (along, across) != (0, 0):
                    block = 2 * (1 - core) + which
                    spot = along * 4 + across
                    landing(which, (along, across), everything, stage3, spot, block).wait_recv()
    loads[2].wait()
    for store in stores:
        store.wait()
    for transfer in sent:
        transfer.wait_send()


def gather_table(tail_t, head_t, rel_t, head_rows, relations):
    blocks, edges = head_rows.shape
    width = head_t.shape[0]
    sems = pltpu.SemaphoreType.DMA
    anywhere = pl.BlockSpec(memory_space=pl.ANY)
    vmem = pl.BlockSpec(memory_space=pltpu.VMEM)
    return pl.pallas_call(
        table_gather,
        out_shape=(
            jax.ShapeDtypeStruct((TAIL,) + tail_t.shape, BF16),
            jax.ShapeDtypeStruct((blocks, width, edges), BF16),
            jax.ShapeDtypeStruct((blocks, width, edges), BF16),
        ),
        in_specs=[anywhere, anywhere, anywhere, vmem, vmem],
        out_specs=(anywhere, anywhere, anywhere),
        scratch_shapes=[
            pltpu.VMEM(head_t.shape, BF16),
            pltpu.VMEM(rel_t.shape, BF16),
            pltpu.VMEM((blocks, width, edges), BF16),
            pltpu.VMEM((blocks, width, edges), BF16),
            sems((2, 4)),
            sems((2, 4)),
            sems((2, 16)),
            sems((2, 16)),
            sems((2, 16)),
            sems((2, 16)),
            sems((3 + 2 * blocks,)),
        ],
        compiler_params=pltpu.CompilerParams(
            collective_id=0, has_side_effects=True, vmem_limit_bytes=40 << 20
        ),
    )(tail_t, head_t, rel_t, head_rows, relations)


def edge_work(
    owners,
    locals_,
    neg_ids,
    live_count,
    table,
    query_hbm,
    rel_hbm,
    head_emb,
    head_state,
    head_rows,
    offsets,
    head_new,
    state_new,
    block_out,
    neg_out,
    chosen,
    neg_t,
    negs,
    query_all,
    rel_all,
    prob_all,
    grad_hi,
    grad_lo,
    hot_all,
    head_grad,
    sems,
):
    blocks, edges = head_rows.shape
    width, rows = head_emb.shape
    half = width // 2
    owned = table.shape[0] // TAIL
    span = chosen.shape[2]
    neg_count = neg_ids.shape[0]
    piece = 160

    fetches = []
    for k in range(neg_count):
        lanes = pl.ds(k * span, span)
        fetches.append(pltpu.make_async_copy(table.at[neg_ids[k]], neg_t.at[:, lanes], sems.at[k]))
    for b in range(blocks):
        block = owners[b] * owned + locals_[b]
        lanes = pl.ds(b * edges, edges)
        spot = neg_count + 3 * b
        fetches.append(
            pltpu.make_async_copy(query_hbm.at[b], query_all.at[:, lanes], sems.at[spot])
        )
        fetches.append(pltpu.make_async_copy(table.at[block], chosen.at[b], sems.at[spot + 1]))
        fetches.append(pltpu.make_async_copy(rel_hbm.at[b], rel_all.at[b], sems.at[spot + 2]))
    for fetch in fetches:
        fetch.start()
    for b in range(blocks):
        hot_all[:, b * edges : (b + 1) * edges] = one_hot(rows, head_rows[b : b + 1, :])
    for fetch in fetches:
        fetch.wait()
    for k in range(neg_count):
        negs[k * span : (k + 1) * span, :] = neg_t[:, k * span : (k + 1) * span].T

    def one_block(b, carry):
        lanes = pl.ds(pl.multiple_of(b * edges, edges), edges)
        live = jnp.where(b < live_count[0], 1.0, 0.0).astype(F32)
        pick = one_hot(span, offsets[pl.ds(b, 1), :])
        tail_vec = mm(chosen[b], pick)
        query = query_all[:, lanes].astype(F32)
        positive = jnp.sum(query * tail_vec, axis=0, keepdims=True)
        score = mm(negs[...], query_all[:, lanes])
        largest = jnp.maximum(positive, jnp.max(score, axis=0, keepdims=True))
        pos_exp = jnp.exp(positive - largest)
        neg_exp = jnp.exp(score - largest)
        denominator = pos_exp + jnp.sum(neg_exp, axis=0, keepdims=True)
        pos_grad = (pos_exp / denominator - 1.0) * live
        prob_all[:, lanes] = (neg_exp * (live / denominator)).astype(BF16)
        query_grad = pos_grad * tail_vec + mm(neg_t[...], prob_all[:, lanes])
        part = pos_grad * query
        part_a = part.astype(BF16)
        rest = part - part_a.astype(F32)
        part_b = rest.astype(BF16)
        part_c = (rest - part_b.astype(F32)).astype(BF16)
        block_grad = mm(pick, part_a, NT) + (mm(pick, part_b, NT) + mm(pick, part_c, NT))
        number = (owners[b] * owned + locals_[b]).astype(F32)
        group = span // HEAD
        for i in range(HEAD):
            block_out[i, b, :, :width] = block_grad[i * group : (i + 1) * group].astype(BF16)
            block_out[i, b, :, width:] = jnp.full((group, LANES - width), number, BF16)
        rel = rel_all[b].astype(F32)
        rr, ri = rel[:half], rel[half:]
        qr, qi = query_grad[:half], query_grad[half:]
        for start, change in ((0, qr * rr + qi * ri), (half, qi * rr - qr * ri)):
            change_hi = change.astype(BF16)
            grad_hi[start : start + half, lanes] = change_hi
            grad_lo[start : start + half, lanes] = (change - change_hi.astype(F32)).astype(BF16)
        return carry

    lax.fori_loop(0, blocks, one_block, 0)

    def neg_rows(k, carry):
        span_rows = pl.ds(pl.multiple_of(k * 256, 256), 256)
        neg_out[span_rows, :] = mm(prob_all[span_rows, :], query_all[...], NT)
        return carry

    lax.fori_loop(0, neg_count * span // 256, neg_rows, 0)

    def head_piece(p, squares):
        spots = pl.ds(pl.multiple_of(p * piece, piece), piece)
        gradient = mm(grad_hi[spots, :], hot_all[...], NT) + mm(grad_lo[spots, :], hot_all[...], NT)
        head_grad[spots, :] = gradient
        return squares + jnp.sum(gradient * gradient, axis=0, keepdims=True)

    squares = lax.fori_loop(0, width // piece, head_piece, jnp.zeros((1, rows), F32))
    state_next = head_state[...] + squares / width
    state_new[...] = state_next
    rate = LEARN_RATE / jnp.sqrt(state_next)

    def head_update(p, carry):
        spots = pl.ds(pl.multiple_of(p * piece, piece), piece)
        head_new[spots, :] = (head_emb[spots, :].astype(F32) - head_grad[spots, :] * rate).astype(
            BF16
        )
        return carry

    lax.fori_loop(0, width // piece, head_update, 0)


def run_edges(
    owners, locals_, neg_ids, live_count, table, query, rel_vec, head_t, head_state, head_rows, offsets
):
    blocks, edges = head_rows.shape
    width, rows = head_t.shape
    span = table.shape[2]
    negs = neg_ids.shape[0]
    total = blocks * edges
    smem = pl.BlockSpec(memory_space=pltpu.SMEM)
    vmem = pl.BlockSpec(memory_space=pltpu.VMEM)
    anywhere = pl.BlockSpec(memory_space=pl.ANY)
    return pl.pallas_call(
        edge_work,
        out_shape=(
            jax.ShapeDtypeStruct((width, rows), BF16),
            jax.ShapeDtypeStruct((1, rows), F32),
            jax.ShapeDtypeStruct((HEAD, blocks, span // HEAD, LANES), BF16),
            jax.ShapeDtypeStruct((negs * span, width), F32),
        ),
        in_specs=[smem, smem, smem, smem, anywhere, anywhere, anywhere] + [vmem] * 4,
        out_specs=(vmem, vmem, vmem, vmem),
        scratch_shapes=[
            pltpu.VMEM((blocks, width, span), BF16),
            pltpu.VMEM((width, negs * span), BF16),
            pltpu.VMEM((negs * span, width), BF16),
            pltpu.VMEM((width, total), BF16),
            pltpu.VMEM((blocks, width, edges), BF16),
            pltpu.VMEM((negs * span, total), BF16),
            pltpu.VMEM((width, total), BF16),
            pltpu.VMEM((width, total), BF16),
            pltpu.VMEM((rows, total), BF16),
            pltpu.VMEM((width, rows), F32),
            pltpu.SemaphoreType.DMA((3 * blocks + negs,)),
        ],
        compiler_params=pltpu.CompilerParams(vmem_limit_bytes=48 << 20),
    )(owners, locals_, neg_ids, live_count, table, query, rel_vec, head_t, head_state, head_rows, offsets)


def remote(source, target, send_sem, recv_sem, device):
    return pltpu.make_async_remote_copy(
        src_ref=source,
        dst_ref=target,
        send_sem=send_sem,
        recv_sem=recv_sem,
        device_id=device,
        device_id_type=MESH,
    )


class PlaneSum:
    def __init__(self, spread, in_x, in_y, mid_x, mid_y, end_x, end_y, sems):
        self.refs = (spread, in_x, in_y, mid_x, mid_y, end_x, end_y)
        self.sems = sems
        self.head, tail = lax.axis_index("head"), lax.axis_index("tail")
        self.col, self.row = lax.rem(tail, SIDE), lax.div(tail, SIDE)

    def steps(self):
        for step in range(1, SIDE):
            col = lax.rem(self.col + step, SIDE)
            row = lax.rem(self.row + step, SIDE)
            yield step - 1, col, row, (self.head, self.row * SIDE + col), (
                self.head,
                row * SIDE + self.col,
            )

    def first(self):
        spread, in_x, in_y = self.refs[:3]
        send, recv = self.sems
        copies = []
        for n, col, row, over_x, over_y in self.steps():
            copies.append(
                remote(spread.at[:, col, pl.ds(0, 2)], in_x.at[n], send.at[n], recv.at[n], over_x)
            )
            copies.append(
                remote(
                    spread.at[row, :, pl.ds(2, 2)], in_y.at[n], send.at[3 + n], recv.at[3 + n], over_y
                )
            )
        return copies

    def second(self):
        mid_x, mid_y, end_x, end_y = self.refs[3:]
        send, recv = self.sems
        copies = []
        for n, col, row, over_x, over_y in self.steps():
            copies.append(remote(mid_x.at[row], end_x.at[n], send.at[6 + n], recv.at[6 + n], over_y))
            copies.append(remote(mid_y.at[col], end_y.at[n], send.at[9 + n], recv.at[9 + n], over_x))
        return copies

    def start_first(self):
        for copy in self.first():
            copy.start()

    def start_second(self):
        spread, in_x, in_y, mid_x, mid_y = self.refs[:5]
        for copy in self.first():
            copy.wait_recv()
        for place in range(SIDE):
            for part in range(2):
                total = spread[place, self.col, part]
                other = spread[self.row, place, 2 + part]
                for n in range(SIDE - 1):
                    total = total + in_x[n, place, part]
                    other = other + in_y[n, place, part]
                mid_x[place, part] = total
                mid_y[place, part] = other
        for copy in self.second():
            copy.start()

    def result(self):
        mid_x, mid_y, end_x, end_y = self.refs[3:]
        for copy in self.second():
            copy.wait_recv()
        parts = []
        for part in range(2):
            total = mid_x[self.row, part]
            for n in range(SIDE - 1):
                total = total + end_x[n, part]
            parts.append(total)
        for part in range(2):
            total = mid_y[self.col, part]
            for n in range(SIDE - 1):
                total = total + end_y[n, part]
            parts.append(total)
        return parts

    def finish(self):
        for copy in self.first() + self.second():
            copy.wait_send()


def exchange(
    neg_ids,
    block_part,
    neg_part,
    own_t,
    own_state,
    out,
    slots,
    theirs,
    mine,
    neg_in_x,
    neg_in_y,
    neg_mid_x,
    neg_mid_y,
    neg_end_x,
    neg_end_y,
    deep,
    deep_in,
    neg_total,
    slot_rows,
    dense,
    in_x,
    in_y,
    mid_x,
    mid_y,
    end_x,
    end_y,
    update,
    sem_bs,
    sem_br,
    sem_cs,
    sem_cr,
    sem_ps,
    sem_pr,
    sem_zs,
    sem_zr,
    sem_ds,
    sem_dr,
    sem_us,
    sem_ur,
    sem_fs,
    sem_fr,
    sem_local,
):
    head, tail = lax.axis_index("head"), lax.axis_index("tail")
    core, depth = lax.rem(head, 2), lax.div(head, 2)
    other = head + 1 - 2 * core
    owned = own_t.shape[0]
    width = own_t.shape[1]
    group = slots.shape[2]
    quarter = DEPTH // 2

    def around(index, step, count):
        return lax.rem(index + step, count)

    keep_block = pltpu.make_async_copy(block_part.at[head], slots.at[head], sem_local.at[0])
    keep_neg = pltpu.make_async_copy(neg_part.at[:, :, :, core], mine, sem_local.at[1])
    keep_neg.start()
    keep_block.start()

    barrier = pltpu.get_barrier_semaphore()

    @pl.loop(1, HEAD)
    def _(step):
        pl.semaphore_signal(
            barrier, inc=1, device_id=(around(head, step, HEAD), tail), device_id_type=MESH
        )
        pl.semaphore_signal(
            barrier, inc=1, device_id=(head, around(tail, step, TAIL)), device_id_type=MESH
        )

    pl.semaphore_wait(barrier, HEAD + TAIL - 2)

    def pair_copy(part):
        return remote(
            neg_part.at[part, :, :, 1 - core],
            theirs.at[part],
            sem_cs.at[part],
            sem_cr.at[part],
            (other, tail),
        )

    for part in range(SIDE):
        pair_copy(part).start()

    def block_copy(step):
        peer = around(head, step, HEAD)
        return remote(
            block_part.at[peer], slots.at[head], sem_bs.at[step], sem_br.at[step], (peer, tail)
        )

    @pl.loop(1, HEAD)
    def _(step):
        block_copy(step).start()

    keep_neg.wait()
    for part in range(SIDE):
        pair_copy(part).wait_recv()
        for place in range(SIDE):
            mine[part, place] = mine[part, place] + theirs[part, place]
    plane = PlaneSum(
        mine, neg_in_x, neg_in_y, neg_mid_x, neg_mid_y, neg_end_x, neg_end_y, (sem_ps, sem_pr)
    )
    plane.start_first()
    plane.start_second()
    for place, total in enumerate(plane.result()):
        deep[place] = total

    zone = lax.rem(tail, 2)
    takes = lax.div(depth, quarter) == zone

    def deep_copy(step):
        level = zone * quarter + step
        return remote(
            deep.at[step],
            deep_in.at[depth],
            sem_zs.at[step],
            sem_zr.at[depth],
            (level * 2 + core, tail),
        )

    def deep_landing(source):
        return remote(
            deep.at[0], deep_in.at[source], sem_zs.at[0], sem_zr.at[source], (other, tail)
        )

    @pl.loop(0, quarter)
    def _(step):
        @pl.when(zone * quarter + step != depth)
        def _():
            deep_copy(step).start()

    neg_total[...] = jnp.zeros_like(neg_total)

    keep_block.wait()

    @pl.loop(1, HEAD)
    def _(step):
        block_copy(step).wait_recv()

    @pl.loop(0, HEAD)
    def _(source):
        for b in range(owned):
            spot = pl.multiple_of((source * owned + b) * group, group)
            slot_rows[pl.ds(spot, group), :] = slots[source, b].astype(F32)

    count = HEAD * owned * group
    number = slot_rows[:, width : width + 1]
    inner = lax.broadcasted_iota(jnp.int32, (count, 1), 0) % group
    goal = number * group + inner.astype(F32)
    spots = lax.broadcasted_iota(jnp.int32, (count, count), 1).astype(F32)
    hot = jnp.where(spots == goal, 1.0, 0.0).astype(BF16)
    sums = mm(hot, slot_rows[:, :width].astype(BF16), TN)

    @pl.when(takes)
    def _():
        deep_in[depth] = deep[depth - zone * quarter]

        @pl.loop(0, DEPTH)
        def _(source):
            @pl.when(source != depth)
            def _():
                deep_landing(source).wait_recv()

        total = deep_in[0]
        for source in range(1, DEPTH):
            total = total + deep_in[source]
        neg_total[...] = total

    target = neg_ids[lax.div(tail, 2)]
    total = neg_total[...]
    for block in range(TAIL * owned):
        y, x, part = block // owned // SIDE, block // owned % SIDE, block % owned
        weight = jnp.where(target == block, 1.0, 0.0).astype(F32)
        dense[y, x, part] = sums[block * group : (block + 1) * group] + weight * total

    table = PlaneSum(dense, in_x, in_y, mid_x, mid_y, end_x, end_y, (sem_ds, sem_dr))
    table.start_first()
    lane = lax.broadcasted_iota(jnp.int32, (group, own_t.shape[2]), 1)
    mark = lane == head * group + lax.broadcasted_iota(jnp.int32, (group, own_t.shape[2]), 0)
    rows_now = [
        mm(jnp.where(mark, 1.0, 0.0).astype(BF16), own_t[b], NT) for b in range(owned)
    ]
    states_now = [
        jnp.sum(jnp.where(mark, own_state[b : b + 1, :], 0.0), axis=1, keepdims=True)
        for b in range(owned)
    ]
    table.start_second()

    for b, gradient in enumerate(table.result()):
        fresh = states_now[b] + jnp.sum(gradient * gradient, axis=1, keepdims=True) / width
        update[b, :, :width] = (
            rows_now[b] - gradient * (LEARN_RATE / jnp.sqrt(fresh))
        ).astype(BF16)
        spot = lax.broadcasted_iota(jnp.int32, (group, LANES - width), 1)
        fresh_a = fresh.astype(BF16).astype(F32)
        fresh_b = (fresh - fresh_a).astype(BF16).astype(F32)
        fresh_c = fresh - fresh_a - fresh_b
        pieces = jnp.where(spot == 0, fresh_a, jnp.where(spot == 1, fresh_b, fresh_c))
        update[b, :, width:] = pieces.astype(BF16)

    def rows_copy(step):
        peer = around(depth, step, DEPTH) * 2 + core
        return remote(update, out.at[:, head], sem_us.at[step], sem_ur.at[step], (peer, tail))

    @pl.loop(1, DEPTH)
    def _(step):
        rows_copy(step).start()

    out_own = pltpu.make_async_copy(update, out.at[:, head], sem_local.at[2])
    out_own.start()
    first_rows = remote(update, out.at[:, head], sem_fs.at[0], sem_fr.at[0], (other, tail))
    first_rows.start()

    def pass_rows(step):
        place = around(depth, DEPTH - step, DEPTH) * 2 + core
        return remote(
            out.at[:, place], out.at[:, place], sem_fs.at[step], sem_fr.at[step], (other, tail)
        )

    @pl.loop(1, DEPTH)
    def _(step):
        rows_copy(step).wait_recv()
        pass_rows(step).start()

    plane.finish()
    table.finish()
    for part in range(SIDE):
        pair_copy(part).wait_send()

    @pl.loop(1, HEAD)
    def _(step):
        block_copy(step).wait_send()

    @pl.loop(0, quarter)
    def _(step):
        @pl.when(zone * quarter + step != depth)
        def _():
            deep_copy(step).wait_send()

    out_own.wait()
    first_rows.wait()

    @pl.loop(1, DEPTH)
    def _(step):
        pass_rows(step).wait()
        rows_copy(step).wait_send()


def run_exchange(neg_ids, block_part, neg_part, own_t, own_state):
    owned, width, span = own_t.shape
    group = span // HEAD
    quarter = DEPTH // 2
    sems = pltpu.SemaphoreType.DMA
    anywhere = pl.BlockSpec(memory_space=pl.ANY)
    vmem = pl.BlockSpec(memory_space=pltpu.VMEM)
    whole = pltpu.VMEM((SIDE, SIDE, 4, group, width), F32)
    plane_sum = (
        [pltpu.VMEM((SIDE - 1, SIDE, 2, group, width), F32)] * 2
        + [pltpu.VMEM((SIDE, 2, group, width), F32)] * 2
        + [pltpu.VMEM((SIDE - 1, 2, group, width), F32)] * 2
    )
    return pl.pallas_call(
        exchange,
        out_shape=jax.ShapeDtypeStruct((owned, HEAD, group, LANES), BF16),
        in_specs=[pl.BlockSpec(memory_space=pltpu.SMEM), anywhere, anywhere, vmem, vmem],
        out_specs=anywhere,
        scratch_shapes=[
            pltpu.VMEM((HEAD, owned, group, LANES), BF16),
            whole,
            whole,
            *plane_sum,
            pltpu.VMEM((quarter, group, width), F32),
            pltpu.VMEM((DEPTH, group, width), F32),
            pltpu.VMEM((group, width), F32),
            pltpu.VMEM((HEAD * owned * group, LANES), F32),
            whole,
            *plane_sum,
            pltpu.VMEM((owned, group, LANES), BF16),
            sems((HEAD,)),
            sems((HEAD,)),
            sems((SIDE,)),
            sems((SIDE,)),
            sems((12,)),
            sems((12,)),
            sems((quarter,)),
            sems((DEPTH,)),
            sems((12,)),
            sems((12,)),
            sems((DEPTH,)),
            sems((DEPTH,)),
            sems((DEPTH,)),
            sems((DEPTH,)),
            sems((3,)),
        ],
        compiler_params=pltpu.CompilerParams(
            collective_id=1, has_side_effects=True, vmem_limit_bytes=48 << 20
        ),
    )(neg_ids, block_part, neg_part, own_t, own_state)


def per_device(
    head_emb,
    head_state,
    tail_emb,
    tail_state,
    relation_emb,
    head_rows,
    relations,
    tail_offsets,
    tail_owner,
    tail_local,
    block_count,
    neg_blocks,
):
    owned, span, width = tail_emb.shape
    group = span // HEAD
    head_t, tail_t = head_emb.T, tail_emb.transpose(0, 2, 1)
    table, query, rel_vec = gather_table(tail_t, head_t, relation_emb.T, head_rows, relations)
    head_new, head_state_new, block_part, neg_part = run_edges(
        tail_owner.reshape(-1),
        tail_local,
        neg_blocks,
        block_count,
        table.reshape(TAIL * owned, width, span),
        query,
        rel_vec,
        head_t,
        head_state[None, :],
        head_rows,
        tail_offsets,
    )
    fresh = run_exchange(
        neg_blocks,
        block_part,
        neg_part.reshape(SIDE, SIDE, DEPTH // 2, 2, group, width),
        tail_t,
        tail_state,
    )
    fresh = fresh.reshape(owned, span, LANES)
    pieces = fresh[:, :, width : width + 3].astype(F32)
    tail_state_new = (pieces[..., 0] + pieces[..., 1]) + pieces[..., 2]
    return (head_new.T, head_state_new[0], fresh[:, :, :width], tail_state_new)


def solution(mesh):
    placed = (
        P(("head", "tail"), None),
        P(("head", "tail")),
        P("tail", None, None),
        P("tail", None),
        P(),
        P(("head", "tail"), None),
        P(("head", "tail"), None),
        P(("head", "tail"), None),
        P(("head", "tail"), None),
        P(("head", "tail")),
        P(("head", "tail")),
        P(),
    )
    return jax.shard_map(
        per_device,
        mesh=mesh,
        in_specs=placed,
        out_specs=(
            P(("head", "tail"), None),
            P(("head", "tail")),
            P("tail", None, None),
            P("tail", None),
        ),
        check_vma=False,
    )
```

time: 185 us -> 146 us (0.79)
  Pallas kernels: 168 us -> 136 us
  local copies, waits for them, and re-layouts: 13.9 us -> 6.6 us
    pallas_call x3, Pallas kernels: 168 us -> 136 us  [the longest x1 65.7 us: run_exchange(): pl.pallas_call(exchange, out_shape=jax.ShapeDtypeStruct((owned, HEAD, gro...]
    unnamed x21 -> x30, local copies, waits for them, and re-layouts: 12.6 us -> 6.5 us
where the time goes in v2:
time: 146 us; the launch traced here: 145 us
  Pallas kernels  136 us (93%)
  local copies, waits for them, and re-layouts  6.6 us (5%)
    pallas_call x1, Pallas kernels, run_exchange(): pl.pallas_call(exchange, out_shape=jax.ShapeDtypeStruct((owned, HEAD, gro...  65.7 us
    pallas_call x1, Pallas kernels, gather_table(): pl.pallas_call(table_gather, out_shape=(jax.ShapeDtypeStruct((TAIL,) + ta...  45.2 us
    pallas_call x1, Pallas kernels, run_edges(): pl.pallas_call(edge_work, out_shape=(jax.ShapeDtypeStruct((width, rows),...  25.3 us
    unnamed x30, local copies, waits for them, and re-layouts  6.5 us

profile of v2, /device:TPU:1, one launch (start us, length us, event | category | flops | bytes accessed | tf_op | source)
XLA Modules:
  0.0 144.8 jit_solution(14256683221274337821)
XLA Ops:
  1.3 0.0 copy-start
  1.3 1.1 copy-done
  2.4 0.0 copy-start.2
  2.4 1.1 copy-done.2
  3.6 0.0 copy-start.4
  3.6 1.4 copy-done.4
  5.0 0.7 copy-done.5
  5.7 0.0 copy-start.7
  5.7 0.7 copy-done.7
  6.4 0.0 copy-start.3
  6.4 0.0 copy-start.6
  6.4 0.0 copy-start.11
  6.4 0.0 copy-start.12
  6.4 0.0 copy-start.13
  6.4 45.2 %shard_map.147 = (bf16[16,4,800,128]{3,2,1,0:T(8,128)(2,1)}, bf16[4,800,256]{2,1,0:T(8,128)(2,1)S(1)}, bf16[4,800,256]{2,1,0:T(8,128)(2,1)S(1)}) custom-call(bf16[4,800,128]{2,1,0:T(8,128)(2,1)S(1)} %bitcast.15, bf16[800,512]{1,0:T(8,128)(2,1)S(1)} %bitcast.17, bf16[800,1024]{1,0:T(8,128)(2,1)S(1)} %bitcast.19, s32[4,256]{1,0:T(4,128)S(1)} %copy-done.5, ...), custom_call_target="tpu_custom_call" | custom-call | tf_op jit(solution)/shard_map/pallas_call | solution.py:205
  51.6 0.0 copy-done.3
  51.6 0.0 copy-done.6
  51.6 0.0 copy-done.8
  51.6 0.0 copy-done.9
  51.6 0.0 copy-done.11
  51.7 0.0 copy-done.12
  51.7 0.0 copy-done.13
  51.7 0.0 copy-start.1
  51.7 0.0 copy-start.10
  51.7 25.3 %shard_map.148 = (bf16[800,512]{1,0:T(8,128)(2,1)}, f32[1,512]{1,0:T(1,128)}, bf16[16,4,8,896]{3,2,1,0:T(8,128)(2,1)S(1)}, f32[1024,800]{1,0:T(8,128)}) custom-call(s32[4]{0:T(128)S(1)} %bitcast.21, s32[4]{0:T(128)S(1)} %copy-done.13, s32[8]{0:T(128)S(1)} %copy-done.11, s32[1]{0:T(128)S(6)} %copy.20.live_count, bf16[64,800,128]{2,1,0:T(8,128)(2,1)} %bitcast.22, ...), custom_call_target="tpu_custom_call" | custom-call | tf_op jit(solution)/shard_map/pallas_call | solution.py:367
  77.0 0.0 copy-done.1
  77.0 0.0 copy-done.10
  77.0 65.7 %shard_map.149 = bf16[4,16,8,896]{3,2,1,0:T(8,128)(2,1)S(1)} custom-call(s32[8]{0:T(128)S(1)} %copy-done.11, bf16[16,4,8,896]{3,2,1,0:T(8,128)(2,1)S(1)} %get-tuple-element.16.block_part, f32[4,4,4,2,8,800]{5,4,3,2,1,0:T(8,128)} %bitcast.23, bf16[4,800,128]{2,1,0:T(8,128)(2,1)S(1)} %bitcast.16, f32[4,128]{1,0:T(4,128)S(1)} %copy-done.10), custom_call_target="tpu_custom_call" | custom-call | tf_op jit(solution)/shard_map/pallas_call | solution.py:749
  142.7 0.1 slice.21
  142.8 0.1 copy.19
  142.9 0.6 fusion
  143.5 1.3 copy.18
  (4 shorter events, 0.0 us)
Async XLA Ops:
  1.3 1.1 copy-start
  2.4 1.1 copy-start.2
  3.6 1.4 copy-start.4
  5.0 0.7 copy-start.5
  5.7 0.7 copy-start.7
  6.4 45.2 %copy-start.3 = (bf16[512,800]{0,1:T(8,128)(2,1)S(1)}, bf16[512,800]{0,1:T(8,128)(2,1)}, u32[]{:S(2)}) copy-start(bf16[512,800]{0,1:T(8,128)(2,1)} %param.12) | copy-start | bytes 2457604
  6.4 45.2 %copy-start.6 = (s32[4,256]{1,0:T(4,128)S(1)}, s32[4,256]{1,0:T(4,128)}, u32[]{:S(2)}) copy-start(s32[4,256]{1,0:T(4,128)} %head_rows.3) | copy-start | bytes 12292
  6.4 45.2 %copy-start.8 = (s32[4,256]{1,0:T(4,128)S(1)}, s32[4,256]{1,0:T(4,128)}, u32[]{:S(2)}) copy-start(s32[4,256]{1,0:T(4,128)} %offsets.1) | copy-start | bytes 12292
  6.4 45.3 %copy-start.9 = (f32[512]{0:T(512)S(1)}, f32[512]{0:T(512)}, u32[]{:S(2)}) copy-start(f32[512]{0:T(512)} %param.13) | copy-start | bytes 6148
  6.4 45.3 %copy-start.11 = (s32[8]{0:T(128)S(1)}, s32[8]{0:T(128)}, u32[]{:S(2)}) copy-start(s32[8]{0:T(128)} %neg_ids.3) | copy-start | bytes 100
  6.4 45.3 %copy-start.12 = (s32[4,1]{0,1:T(1,128)S(1)}, s32[4,1]{0,1:T(1,128)}, u32[]{:S(2)}) copy-start(s32[4,1]{0,1:T(1,128)} %param.20) | copy-start | bytes 52
  6.4 45.3 %copy-start.13 = (s32[4]{0:T(128)S(1)}, s32[4]{0:T(128)}, u32[]{:S(2)}) copy-start(s32[4]{0:T(128)} %locals_.1) | copy-start | bytes 52
  51.7 25.3 %copy-start.1 = (bf16[4,128,800]{1,2,0:T(8,128)(2,1)S(1)}, bf16[4,128,800]{1,2,0:T(8,128)(2,1)}, u32[]{:S(2)}) copy-start(bf16[4,128,800]{1,2,0:T(8,128)(2,1)} %param.14) | copy-start | bytes 2457604
  51.7 25.3 %copy-start.10 = (f32[4,128]{1,0:T(4,128)S(1)}, f32[4,128]{1,0:T(4,128)}, u32[]{:S(2)}) copy-start(f32[4,128]{1,0:T(4,128)} %own_state.1) | copy-start | bytes 6148

commit v3 on v2

--- a/solution.py
+++ b/solution.py
@@ -14,6 +14,7 @@
 HEAD = 16
 TAIL = 16
 LANES = 896
+VMEM_BYTES = 64 << 20
 
 
 def greet(targets):
@@ -40,13 +41,15 @@
     own,
     head_hbm,
     rel_hbm,
-    head_rows,
-    relations,
+    head_rows_hbm,
+    relations_hbm,
     table,
     query_out,
     rel_out,
     head_t,
     rel_t,
+    head_rows,
+    relations,
     query,
     rel_vec,
     send1,
@@ -69,6 +72,8 @@
         pltpu.make_async_copy(head_hbm, head_t, local.at[0]),
         pltpu.make_async_copy(rel_hbm, rel_t, local.at[1]),
         pltpu.make_async_copy(own, table.at[tail], local.at[2]),
+        pltpu.make_async_copy(head_rows_hbm, head_rows, local.at[3 + 2 * blocks]),
+        pltpu.make_async_copy(relations_hbm, relations, local.at[4 + 2 * blocks]),
     ]
     for load in loads:
         load.start()
@@ -146,8 +151,8 @@
         send(which, (0, 0), everything, stage1, 1, (head, place(which, -1, 0)))
     for which in (0, 1):
         spread(which, (0, 0))
-    loads[0].wait()
-    loads[1].wait()
+    for n in (0, 1, 3, 4):
+        loads[n].wait()
     make_query(0)
     for which in (0, 1):
         landing(which, (-1, 0), everything, stage1, 0).wait_recv()
@@ -201,7 +206,6 @@
     width = head_t.shape[0]
     sems = pltpu.SemaphoreType.DMA
     anywhere = pl.BlockSpec(memory_space=pl.ANY)
-    vmem = pl.BlockSpec(memory_space=pltpu.VMEM)
     return pl.pallas_call(
         table_gather,
         out_shape=(
@@ -209,11 +213,13 @@
             jax.ShapeDtypeStruct((blocks, width, edges), BF16),
             jax.ShapeDtypeStruct((blocks, width, edges), BF16),
         ),
-        in_specs=[anywhere, anywhere, anywhere, vmem, vmem],
+        in_specs=[pl.BlockSpec(memory_space=pltpu.HBM)] * 5,
         out_specs=(anywhere, anywhere, anywhere),
         scratch_shapes=[
             pltpu.VMEM(head_t.shape, BF16),
             pltpu.VMEM(rel_t.shape, BF16),
+            pltpu.VMEM(head_rows.shape, jnp.int32),
+            pltpu.VMEM(relations.shape, jnp.int32),
             pltpu.VMEM((blocks, width, edges), BF16),
             pltpu.VMEM((blocks, width, edges), BF16),
             sems((2, 4)),
@@ -222,10 +228,10 @@
             sems((2, 16)),
             sems((2, 16)),
             sems((2, 16)),
-            sems((3 + 2 * blocks,)),
+            sems((5 + 2 * blocks,)),
         ],
         compiler_params=pltpu.CompilerParams(
-            collective_id=0, has_side_effects=True, vmem_limit_bytes=40 << 20
+            collective_id=0, has_side_effects=True, vmem_limit_bytes=VMEM_BYTES
         ),
     )(tail_t, head_t, rel_t, head_rows, relations)
 
@@ -238,33 +244,26 @@
     table,
     query_hbm,
     rel_hbm,
-    head_emb,
-    head_state,
-    head_rows,
     offsets,
-    head_new,
-    state_new,
     block_out,
-    neg_out,
+    prob_out,
+    grad_out,
     chosen,
     neg_t,
     negs,
     query_all,
     rel_all,
-    prob_all,
-    grad_hi,
-    grad_lo,
-    hot_all,
-    head_grad,
+    prob,
+    grad,
     sems,
 ):
-    blocks, edges = head_rows.shape
-    width, rows = head_emb.shape
+    blocks, edges = offsets.shape
+    width = neg_t.shape[0]
     half = width // 2
     owned = table.shape[0] // TAIL
     span = chosen.shape[2]
+    group = span // HEAD
     neg_count = neg_ids.shape[0]
-    piece = 160
 
     fetches = []
     for k in range(neg_count):
@@ -272,37 +271,39 @@
         fetches.append(pltpu.make_async_copy(table.at[neg_ids[k]], neg_t.at[:, lanes], sems.at[k]))
     for b in range(blocks):
         block = owners[b] * owned + locals_[b]
-        lanes = pl.ds(b * edges, edges)
         spot = neg_count + 3 * b
-        fetches.append(
-            pltpu.make_async_copy(query_hbm.at[b], query_all.at[:, lanes], sems.at[spot])
-        )
+        fetches.append(pltpu.make_async_copy(query_hbm.at[b], query_all.at[b], sems.at[spot]))
         fetches.append(pltpu.make_async_copy(table.at[block], chosen.at[b], sems.at[spot + 1]))
         fetches.append(pltpu.make_async_copy(rel_hbm.at[b], rel_all.at[b], sems.at[spot + 2]))
     for fetch in fetches:
         fetch.start()
-    for b in range(blocks):
-        hot_all[:, b * edges : (b + 1) * edges] = one_hot(rows, head_rows[b : b + 1, :])
-    for fetch in fetches:
+    for k in range(neg_count):
+        fetches[k].wait()
+        negs[k * span : (k + 1) * span, :] = neg_t[:, k * span : (k + 1) * span].T
+    for fetch in fetches[neg_count:]:
         fetch.wait()
-    for k in range(neg_count):
-        negs[k * span : (k + 1) * span, :] = neg_t[:, k * span : (k + 1) * span].T
+
+    def results(b):
+        spot = neg_count + 3 * blocks
+        return [
+            pltpu.make_async_copy(prob.at[b], prob_out.at[b], sems.at[spot + b]),
+            pltpu.make_async_copy(grad.at[b], grad_out.at[b], sems.at[spot + blocks + b]),
+        ]
 
     def one_block(b, carry):
-        lanes = pl.ds(pl.multiple_of(b * edges, edges), edges)
         live = jnp.where(b < live_count[0], 1.0, 0.0).astype(F32)
         pick = one_hot(span, offsets[pl.ds(b, 1), :])
         tail_vec = mm(chosen[b], pick)
-        query = query_all[:, lanes].astype(F32)
+        query = query_all[b].astype(F32)
         positive = jnp.sum(query * tail_vec, axis=0, keepdims=True)
-        score = mm(negs[...], query_all[:, lanes])
+        score = mm(negs[...], query_all[b])
         largest = jnp.maximum(positive, jnp.max(score, axis=0, keepdims=True))
         pos_exp = jnp.exp(positive - largest)
         neg_exp = jnp.exp(score - largest)
         denominator = pos_exp + jnp.sum(neg_exp, axis=0, keepdims=True)
         pos_grad = (pos_exp / denominator - 1.0) * live
-        prob_all[:, lanes] = (neg_exp * (live / denominator)).astype(BF16)
-        query_grad = pos_grad * tail_vec + mm(neg_t[...], prob_all[:, lanes])
+        prob[b] = (neg_exp * (live / denominator)).astype(BF16)
+        query_grad = pos_grad * tail_vec + mm(neg_t[...], prob[b])
         part = pos_grad * query
         part_a = part.astype(BF16)
         rest = part - part_a.astype(F32)
@@ -310,7 +311,6 @@
         part_c = (rest - part_b.astype(F32)).astype(BF16)
         block_grad = mm(pick, part_a, NT) + (mm(pick, part_b, NT) + mm(pick, part_c, NT))
         number = (owners[b] * owned + locals_[b]).astype(F32)
-        group = span // HEAD
         for i in range(HEAD):
             block_out[i, b, :, :width] = block_grad[i * group : (i + 1) * group].astype(BF16)
             block_out[i, b, :, width:] = jnp.full((group, LANES - width), number, BF16)
@@ -319,76 +319,46 @@
         qr, qi = query_grad[:half], query_grad[half:]
         for start, change in ((0, qr * rr + qi * ri), (half, qi * rr - qr * ri)):
             change_hi = change.astype(BF16)
-            grad_hi[start : start + half, lanes] = change_hi
-            grad_lo[start : start + half, lanes] = (change - change_hi.astype(F32)).astype(BF16)
+            grad[b, 0, start : start + half, :] = change_hi
+            grad[b, 1, start : start + half, :] = (change - change_hi.astype(F32)).astype(BF16)
+        for result in results(b):
+            result.start()
         return carry
 
     lax.fori_loop(0, blocks, one_block, 0)
-
-    def neg_rows(k, carry):
-        span_rows = pl.ds(pl.multiple_of(k * 256, 256), 256)
-        neg_out[span_rows, :] = mm(prob_all[span_rows, :], query_all[...], NT)
-        return carry
-
-    lax.fori_loop(0, neg_count * span // 256, neg_rows, 0)
-
-    def head_piece(p, squares):
-        spots = pl.ds(pl.multiple_of(p * piece, piece), piece)
-        gradient = mm(grad_hi[spots, :], hot_all[...], NT) + mm(grad_lo[spots, :], hot_all[...], NT)
-        head_grad[spots, :] = gradient
-        return squares + jnp.sum(gradient * gradient, axis=0, keepdims=True)
-
-    squares = lax.fori_loop(0, width // piece, head_piece, jnp.zeros((1, rows), F32))
-    state_next = head_state[...] + squares / width
-    state_new[...] = state_next
-    rate = LEARN_RATE / jnp.sqrt(state_next)
-
-    def head_update(p, carry):
-        spots = pl.ds(pl.multiple_of(p * piece, piece), piece)
-        head_new[spots, :] = (head_emb[spots, :].astype(F32) - head_grad[spots, :] * rate).astype(
-            BF16
-        )
-        return carry
-
-    lax.fori_loop(0, width // piece, head_update, 0)
-
-
-def run_edges(
-    owners, locals_, neg_ids, live_count, table, query, rel_vec, head_t, head_state, head_rows, offsets
-):
-    blocks, edges = head_rows.shape
-    width, rows = head_t.shape
-    span = table.shape[2]
+    for b in range(blocks):
+        for result in results(b):
+            result.wait()
+
+
+def run_edges(owners, locals_, neg_ids, live_count, table, query, rel_vec, offsets):
+    blocks, edges = offsets.shape
+    width, span = table.shape[1:]
     negs = neg_ids.shape[0]
-    total = blocks * edges
     smem = pl.BlockSpec(memory_space=pltpu.SMEM)
     vmem = pl.BlockSpec(memory_space=pltpu.VMEM)
     anywhere = pl.BlockSpec(memory_space=pl.ANY)
     return pl.pallas_call(
         edge_work,
         out_shape=(
-            jax.ShapeDtypeStruct((width, rows), BF16),
-            jax.ShapeDtypeStruct((1, rows), F32),
             jax.ShapeDtypeStruct((HEAD, blocks, span // HEAD, LANES), BF16),
-            jax.ShapeDtypeStruct((negs * span, width), F32),
+            jax.ShapeDtypeStruct((blocks, negs * span, edges), BF16),
+            jax.ShapeDtypeStruct((blocks, 2, width, edges), BF16),
         ),
-        in_specs=[smem, smem, smem, smem, anywhere, anywhere, anywhere] + [vmem] * 4,
-        out_specs=(vmem, vmem, vmem, vmem),
+        in_specs=[smem, smem, smem, smem, anywhere, anywhere, anywhere, vmem],
+        out_specs=(vmem, anywhere, anywhere),
         scratch_shapes=[
             pltpu.VMEM((blocks, width, span), BF16),
             pltpu.VMEM((width, negs * span), BF16),
             pltpu.VMEM((negs * span, width), BF16),
-            pltpu.VMEM((width, total), BF16),
             pltpu.VMEM((blocks, width, edges), BF16),
-            pltpu.VMEM((negs * span, total), BF16),
-            pltpu.VMEM((width, total), BF16),
-            pltpu.VMEM((width, total), BF16),
-            pltpu.VMEM((rows, total), BF16),
-            pltpu.VMEM((width, rows), F32),
-            pltpu.SemaphoreType.DMA((3 * blocks + negs,)),
+            pltpu.VMEM((blocks, width, edges), BF16),
+            pltpu.VMEM((blocks, negs * span, edges), BF16),
+            pltpu.VMEM((blocks, 2, width, edges), BF16),
+            pltpu.SemaphoreType.DMA((5 * blocks + negs,)),
         ],
-        compiler_params=pltpu.CompilerParams(vmem_limit_bytes=48 << 20),
-    )(owners, locals_, neg_ids, live_count, table, query, rel_vec, head_t, head_state, head_rows, offsets)
+        compiler_params=pltpu.CompilerParams(vmem_limit_bytes=VMEM_BYTES),
+    )(owners, locals_, neg_ids, live_count, table, query, rel_vec, offsets)
 
 
 def remote(source, target, send_sem, recv_sem, device):
@@ -487,10 +457,24 @@
 def exchange(
     neg_ids,
     block_part,
-    neg_part,
+    prob_hbm,
+    query_hbm,
+    grad_hbm,
+    head_hbm,
+    head_rows,
+    head_state,
     own_t,
     own_state,
     out,
+    head_new,
+    state_new,
+    prob,
+    query,
+    grad,
+    head_emb,
+    head_grad,
+    hot_head,
+    neg_part,
     slots,
     theirs,
     mine,
@@ -540,8 +524,14 @@
         return lax.rem(index + step, count)
 
     keep_block = pltpu.make_async_copy(block_part.at[head], slots.at[head], sem_local.at[0])
-    keep_neg = pltpu.make_async_copy(neg_part.at[:, :, :, core], mine, sem_local.at[1])
-    keep_neg.start()
+    loads = [
+        pltpu.make_async_copy(prob_hbm, prob, sem_local.at[1]),
+        pltpu.make_async_copy(query_hbm, query, sem_local.at[3]),
+        pltpu.make_async_copy(grad_hbm, grad, sem_local.at[4]),
+        pltpu.make_async_copy(head_hbm, head_emb, sem_local.at[5]),
+    ]
+    for load in loads:
+        load.start()
     keep_block.start()
 
     barrier = pltpu.get_barrier_semaphore()
@@ -555,6 +545,19 @@
             barrier, inc=1, device_id=(head, around(tail, step, TAIL)), device_id_type=MESH
         )
 
+    loads[0].wait()
+    loads[1].wait()
+    blocks = prob.shape[0]
+    chunk = prob.shape[1] // SIDE
+
+    @pl.loop(0, SIDE)
+    def _(part):
+        spots = pl.ds(pl.multiple_of(part * chunk, chunk), chunk)
+        total = mm(prob[0, spots, :], query[0], NT)
+        for b in range(1, blocks):
+            total = total + mm(prob[b, spots, :], query[b], NT)
+        neg_part[part] = total.reshape(neg_part.shape[1:])
+
     pl.semaphore_wait(barrier, HEAD + TAIL - 2)
 
     def pair_copy(part):
@@ -579,16 +582,47 @@
     def _(step):
         block_copy(step).start()
 
-    keep_neg.wait()
     for part in range(SIDE):
         pair_copy(part).wait_recv()
         for place in range(SIDE):
-            mine[part, place] = mine[part, place] + theirs[part, place]
+            mine[part, place] = neg_part[part, place, :, core] + theirs[part, place]
     plane = PlaneSum(
         mine, neg_in_x, neg_in_y, neg_mid_x, neg_mid_y, neg_end_x, neg_end_y, (sem_ps, sem_pr)
     )
     plane.start_first()
+
+    loads[2].wait()
+    loads[3].wait()
+    rows, edges = hot_head.shape[0], head_rows.shape[1]
+    piece = 160
+    for b in range(blocks):
+        hot_head[:, b * edges : (b + 1) * edges] = one_hot(rows, head_rows[b : b + 1, :])
+
+    def head_piece(p, squares):
+        spots = pl.ds(pl.multiple_of(p * piece, piece), piece)
+        gradient = jnp.zeros((piece, rows), F32)
+        for b in range(blocks):
+            lanes = slice(b * edges, (b + 1) * edges)
+            for n in range(2):
+                gradient = gradient + mm(grad[b, n, spots, :], hot_head[:, lanes], NT)
+        head_grad[spots, :] = gradient
+        return squares + jnp.sum(gradient * gradient, axis=0, keepdims=True)
+
+    squares = lax.fori_loop(0, width // piece, head_piece, jnp.zeros((1, rows), F32))
     plane.start_second()
+    head_next = head_state[...] + squares / width
+    state_new[...] = head_next
+    rate = LEARN_RATE / jnp.sqrt(head_next)
+
+    @pl.loop(0, width // piece)
+    def _(p):
+        spots = pl.ds(pl.multiple_of(p * piece, piece), piece)
+        head_emb[spots, :] = (head_emb[spots, :].astype(F32) - head_grad[spots, :] * rate).astype(
+            BF16
+        )
+
+    head_store = pltpu.make_async_copy(head_emb, head_new, sem_local.at[6])
+    head_store.start()
     for place, total in enumerate(plane.result()):
         deep[place] = total
 
@@ -725,6 +759,7 @@
             deep_copy(step).wait_send()
 
     out_own.wait()
+    head_store.wait()
     first_rows.wait()
 
     @pl.loop(1, DEPTH)
@@ -733,7 +768,11 @@
         rows_copy(step).wait_send()
 
 
-def run_exchange(neg_ids, block_part, neg_part, own_t, own_state):
+def run_exchange(
+    neg_ids, block_part, prob, query, grad, head_t, head_rows, head_state, own_t, own_state
+):
+    rows = head_t.shape[1]
+    total = head_rows.shape[0] * head_rows.shape[1]
     owned, width, span = own_t.shape
     group = span // HEAD
     quarter = DEPTH // 2
@@ -748,10 +787,24 @@
     )
     return pl.pallas_call(
         exchange,
-        out_shape=jax.ShapeDtypeStruct((owned, HEAD, group, LANES), BF16),
-        in_specs=[pl.BlockSpec(memory_space=pltpu.SMEM), anywhere, anywhere, vmem, vmem],
-        out_specs=anywhere,
+        out_shape=(
+            jax.ShapeDtypeStruct((owned, HEAD, group, LANES), BF16),
+            jax.ShapeDtypeStruct(head_t.shape, BF16),
+            jax.ShapeDtypeStruct((1, rows), F32),
+        ),
+        in_specs=[pl.BlockSpec(memory_space=pltpu.SMEM)]
+        + [anywhere] * 4
+        + [pl.BlockSpec(memory_space=pltpu.HBM)]
+        + [vmem] * 4,
+        out_specs=(anywhere, anywhere, vmem),
         scratch_shapes=[
+            pltpu.VMEM(prob.shape, BF16),
+            pltpu.VMEM(query.shape, BF16),
+            pltpu.VMEM(grad.shape, BF16),
+            pltpu.VMEM(head_t.shape, BF16),
+            pltpu.VMEM(head_t.shape, F32),
+            pltpu.VMEM((rows, total), BF16),
+            pltpu.VMEM((SIDE, SIDE, 4, 2, group, width), F32),
             pltpu.VMEM((HEAD, owned, group, LANES), BF16),
             whole,
             whole,
@@ -777,12 +830,12 @@
             sems((DEPTH,)),
             sems((DEPTH,)),
             sems((DEPTH,)),
-            sems((3,)),
+            sems((7,)),
         ],
         compiler_params=pltpu.CompilerParams(
-            collective_id=1, has_side_effects=True, vmem_limit_bytes=48 << 20
+            collective_id=1, has_side_effects=True, vmem_limit_bytes=VMEM_BYTES
         ),
-    )(neg_ids, block_part, neg_part, own_t, own_state)
+    )(neg_ids, block_part, prob, query, grad, head_t, head_rows, head_state, own_t, own_state)
 
 
 def per_device(
@@ -800,10 +853,9 @@
     neg_blocks,
 ):
     owned, span, width = tail_emb.shape
-    group = span // HEAD
     head_t, tail_t = head_emb.T, tail_emb.transpose(0, 2, 1)
     table, query, rel_vec = gather_table(tail_t, head_t, relation_emb.T, head_rows, relations)
-    head_new, head_state_new, block_part, neg_part = run_edges(
+    block_part, prob, grad = run_edges(
         tail_owner.reshape(-1),
         tail_local,
         neg_blocks,
@@ -811,15 +863,17 @@
         table.reshape(TAIL * owned, width, span),
         query,
         rel_vec,
-        head_t,
-        head_state[None, :],
-        head_rows,
         tail_offsets,
     )
-    fresh = run_exchange(
+    fresh, head_new, head_state_new = run_exchange(
         neg_blocks,
         block_part,
-        neg_part.reshape(SIDE, SIDE, DEPTH // 2, 2, group, width),
+        prob,
+        query,
+        grad,
+        head_t,
+        head_rows,
+        head_state[None, :],
         tail_t,
         tail_state,
     )

time: 146 us -> 139 us (0.952)
  Pallas kernels: 136 us -> 132 us
  local copies, waits for them, and re-layouts: 6.6 us -> 4.85 us
    pallas_call x2, Pallas kernels: 90.9 us -> 87.2 us  [the longest x1 69.6 us: run_exchange(): pl.pallas_call(exchange, out_shape=(jax.ShapeDtypeStruct((owned, HEAD, gr...]
    unnamed x30 -> x8, local copies, waits for them, and re-layouts: 6.5 us -> 3.78 us
where the time goes in v3:
time: 139 us
  Pallas kernels  132 us (95%)
  local copies, waits for them, and re-layouts  4.85 us (3%)
    pallas_call x1, Pallas kernels, run_exchange(): pl.pallas_call(exchange, out_shape=(jax.ShapeDtypeStruct((owned, HEAD, gr...  69.6 us
    pallas_call x1, Pallas kernels, gather_table(): pl.pallas_call(table_gather, out_shape=(jax.ShapeDtypeStruct((TAIL,) + ta...  45.1 us
    pallas_call x1, Pallas kernels, run_edges(): pl.pallas_call(edge_work, out_shape=(jax.ShapeDtypeStruct((HEAD, blocks,...  17.6 us
    unnamed x8, local copies, waits for them, and re-layouts  3.78 us

profile of v3, /device:TPU:1, one launch (start us, length us, event | category | flops | bytes accessed | tf_op | source)
XLA Modules:
  0.0 139.1 jit_solution(8018433100673445254)
XLA Ops:
  1.3 45.1 %shard_map.147 = (bf16[16,4,800,128]{3,2,1,0:T(8,128)(2,1)}, bf16[4,800,256]{2,1,0:T(8,128)(2,1)}, bf16[4,800,256]{2,1,0:T(8,128)(2,1)}) custom-call(bf16[4,800,128]{2,1,0:T(8,128)(2,1)} %bitcast.13, bf16[800,512]{1,0:T(8,128)(2,1)} %bitcast.15, bf16[800,1024]{1,0:T(8,128)(2,1)} %bitcast.17, s32[4,256]{1,0:T(4,128)} %head_rows.1, s32[4,256]{1,0:T(4,128)} %relations_hbm.1), custom_call_target="tpu_custom_call" | custom-call | tf_op jit(solution)/shard_map/pallas_call | solution.py:209
  46.4 17.6 %shard_map.148 = (bf16[16,4,8,896]{3,2,1,0:T(8,128)(2,1)}, bf16[4,1024,256]{2,1,0:T(8,128)(2,1)}, bf16[4,2,800,256]{3,2,1,0:T(8,128)(2,1)}) custom-call(s32[4]{0:T(128)} %bitcast.23, s32[4]{0:T(128)} %locals_.1, s32[8]{0:T(128)} %neg_ids.3, s32[1]{0:T(128)S(6)} %copy.22.live_count, bf16[64,800,128]{2,1,0:T(8,128)(2,1)} %bitcast.12, ...), custom_call_target="tpu_custom_call" | custom-call | tf_op jit(solution)/shard_map/pallas_call | solution.py:341
  64.0 69.6 %shard_map.149 = (bf16[4,16,8,896]{3,2,1,0:T(8,128)(2,1)}, bf16[800,512]{1,0:T(8,128)(2,1)}, f32[1,512]{1,0:T(1,128)}) custom-call(s32[8]{0:T(128)} %neg_ids.3, bf16[16,4,8,896]{3,2,1,0:T(8,128)(2,1)} %get-tuple-element.16.block_part, bf16[4,1024,256]{2,1,0:T(8,128)(2,1)} %get-tuple-element.17.prob_hbm, bf16[4,800,256]{2,1,0:T(8,128)(2,1)} %get-tuple-element.14.query_hbm, ...), custom_call_target="tpu_custom_call" | custom-call | tf_op jit(solution)/shard_map/pallas_call | solution.py:788
  133.6 0.0 copy-start
  133.6 0.0 copy-start.1
  133.6 1.1 slice.21
  134.7 0.1 copy.19
  134.8 0.6 fusion
  135.4 2.2 %copy.18 = bf16[4,128,800]{1,2,0:T(8,128)(2,1)} copy(bf16[4,128,800]{2,1,0:T(8,128)(2,1)} %bitcast.19) | data formatting | bytes 1638400
  137.6 0.0 copy-done
  137.6 0.9 copy.23
  138.5 0.0 copy-done.1
  138.5 0.6 copy.24
  (1 shorter events, 0.0 us)
Async XLA Ops:
  133.6 4.0 %copy-start = (bf16[800,512]{1,0:T(8,128)(2,1)S(1)}, bf16[800,512]{1,0:T(8,128)(2,1)}, u32[]{:S(2)}) copy-start(bf16[800,512]{1,0:T(8,128)(2,1)} %get-tuple-element.19) | copy-start | bytes 2457604
  133.6 4.9 %copy-start.1 = (f32[1,512]{1,0:T(1,128)S(1)}, f32[1,512]{1,0:T(1,128)}, u32[]{:S(2)}) copy-start(f32[1,512]{1,0:T(1,128)} %get-tuple-element.20) | copy-start | bytes 6148

commit v4 on v3

--- a/solution.py
+++ b/solution.py
@@ -13,6 +13,7 @@
 DEPTH = 8
 HEAD = 16
 TAIL = 16
+CUT = 512
 LANES = 896
 VMEM_BYTES = 64 << 20
 
@@ -236,129 +237,39 @@
     )(tail_t, head_t, rel_t, head_rows, relations)
 
 
-def edge_work(
-    owners,
-    locals_,
-    neg_ids,
-    live_count,
-    table,
-    query_hbm,
-    rel_hbm,
-    offsets,
-    block_out,
-    prob_out,
-    grad_out,
-    chosen,
-    neg_t,
-    negs,
-    query_all,
-    rel_all,
-    prob,
-    grad,
-    sems,
-):
-    blocks, edges = offsets.shape
-    width = neg_t.shape[0]
-    half = width // 2
+def pick_blocks(owners, locals_, neg_ids, table, chosen, neg_t, sems):
     owned = table.shape[0] // TAIL
-    span = chosen.shape[2]
-    group = span // HEAD
-    neg_count = neg_ids.shape[0]
-
-    fetches = []
-    for k in range(neg_count):
+    span = table.shape[2]
+    copies = []
+    for k in range(neg_ids.shape[0]):
         lanes = pl.ds(k * span, span)
-        fetches.append(pltpu.make_async_copy(table.at[neg_ids[k]], neg_t.at[:, lanes], sems.at[k]))
-    for b in range(blocks):
+        copies.append(pltpu.make_async_copy(table.at[neg_ids[k]], neg_t.at[:, lanes], sems.at[k]))
+    for b in range(chosen.shape[0]):
         block = owners[b] * owned + locals_[b]
-        spot = neg_count + 3 * b
-        fetches.append(pltpu.make_async_copy(query_hbm.at[b], query_all.at[b], sems.at[spot]))
-        fetches.append(pltpu.make_async_copy(table.at[block], chosen.at[b], sems.at[spot + 1]))
-        fetches.append(pltpu.make_async_copy(rel_hbm.at[b], rel_all.at[b], sems.at[spot + 2]))
-    for fetch in fetches:
-        fetch.start()
-    for k in range(neg_count):
-        fetches[k].wait()
-        negs[k * span : (k + 1) * span, :] = neg_t[:, k * span : (k + 1) * span].T
-    for fetch in fetches[neg_count:]:
-        fetch.wait()
-
-    def results(b):
-        spot = neg_count + 3 * blocks
-        return [
-            pltpu.make_async_copy(prob.at[b], prob_out.at[b], sems.at[spot + b]),
-            pltpu.make_async_copy(grad.at[b], grad_out.at[b], sems.at[spot + blocks + b]),
-        ]
-
-    def one_block(b, carry):
-        live = jnp.where(b < live_count[0], 1.0, 0.0).astype(F32)
-        pick = one_hot(span, offsets[pl.ds(b, 1), :])
-        tail_vec = mm(chosen[b], pick)
-        query = query_all[b].astype(F32)
-        positive = jnp.sum(query * tail_vec, axis=0, keepdims=True)
-        score = mm(negs[...], query_all[b])
-        largest = jnp.maximum(positive, jnp.max(score, axis=0, keepdims=True))
-        pos_exp = jnp.exp(positive - largest)
-        neg_exp = jnp.exp(score - largest)
-        denominator = pos_exp + jnp.sum(neg_exp, axis=0, keepdims=True)
-        pos_grad = (pos_exp / denominator - 1.0) * live
-        prob[b] = (neg_exp * (live / denominator)).astype(BF16)
-        query_grad = pos_grad * tail_vec + mm(neg_t[...], prob[b])
-        part = pos_grad * query
-        part_a = part.astype(BF16)
-        rest = part - part_a.astype(F32)
-        part_b = rest.astype(BF16)
-        part_c = (rest - part_b.astype(F32)).astype(BF16)
-        block_grad = mm(pick, part_a, NT) + (mm(pick, part_b, NT) + mm(pick, part_c, NT))
-        number = (owners[b] * owned + locals_[b]).astype(F32)
-        for i in range(HEAD):
-            block_out[i, b, :, :width] = block_grad[i * group : (i + 1) * group].astype(BF16)
-            block_out[i, b, :, width:] = jnp.full((group, LANES - width), number, BF16)
-        rel = rel_all[b].astype(F32)
-        rr, ri = rel[:half], rel[half:]
-        qr, qi = query_grad[:half], query_grad[half:]
-        for start, change in ((0, qr * rr + qi * ri), (half, qi * rr - qr * ri)):
-            change_hi = change.astype(BF16)
-            grad[b, 0, start : start + half, :] = change_hi
-            grad[b, 1, start : start + half, :] = (change - change_hi.astype(F32)).astype(BF16)
-        for result in results(b):
-            result.start()
-        return carry
-
-    lax.fori_loop(0, blocks, one_block, 0)
-    for b in range(blocks):
-        for result in results(b):
-            result.wait()
-
-
-def run_edges(owners, locals_, neg_ids, live_count, table, query, rel_vec, offsets):
-    blocks, edges = offsets.shape
+        spot = neg_ids.shape[0] + b
+        copies.append(pltpu.make_async_copy(table.at[block], chosen.at[b], sems.at[spot]))
+    for copy in copies:
+        copy.start()
+    for copy in copies:
+        copy.wait()
+
+
+def run_pick(owners, locals_, neg_ids, table):
+    blocks, negs = owners.shape[0], neg_ids.shape[0]
     width, span = table.shape[1:]
-    negs = neg_ids.shape[0]
     smem = pl.BlockSpec(memory_space=pltpu.SMEM)
-    vmem = pl.BlockSpec(memory_space=pltpu.VMEM)
     anywhere = pl.BlockSpec(memory_space=pl.ANY)
     return pl.pallas_call(
-        edge_work,
+        pick_blocks,
         out_shape=(
-            jax.ShapeDtypeStruct((HEAD, blocks, span // HEAD, LANES), BF16),
-            jax.ShapeDtypeStruct((blocks, negs * span, edges), BF16),
-            jax.ShapeDtypeStruct((blocks, 2, width, edges), BF16),
+            jax.ShapeDtypeStruct((blocks, width, span), BF16),
+            jax.ShapeDtypeStruct((width, negs * span), BF16),
         ),
-        in_specs=[smem, smem, smem, smem, anywhere, anywhere, anywhere, vmem],
-        out_specs=(vmem, anywhere, anywhere),
-        scratch_shapes=[
-            pltpu.VMEM((blocks, width, span), BF16),
-            pltpu.VMEM((width, negs * span), BF16),
-            pltpu.VMEM((negs * span, width), BF16),
-            pltpu.VMEM((blocks, width, edges), BF16),
-            pltpu.VMEM((blocks, width, edges), BF16),
-            pltpu.VMEM((blocks, negs * span, edges), BF16),
-            pltpu.VMEM((blocks, 2, width, edges), BF16),
-            pltpu.SemaphoreType.DMA((5 * blocks + negs,)),
-        ],
+        in_specs=[smem, smem, smem, anywhere],
+        out_specs=(anywhere, anywhere),
+        scratch_shapes=[pltpu.SemaphoreType.DMA((blocks + negs,))],
         compiler_params=pltpu.CompilerParams(vmem_limit_bytes=VMEM_BYTES),
-    )(owners, locals_, neg_ids, live_count, table, query, rel_vec, offsets)
+    )(owners, locals_, neg_ids, table)
 
 
 def remote(source, target, send_sem, recv_sem, device):
@@ -455,12 +366,16 @@
 
 
 def exchange(
+    owners,
+    locals_,
+    live_count,
     neg_ids,
-    block_part,
-    prob_hbm,
+    chosen_hbm,
+    neg_hbm,
     query_hbm,
-    grad_hbm,
+    rel_hbm,
     head_hbm,
+    offsets,
     head_rows,
     head_state,
     own_t,
@@ -468,9 +383,14 @@
     out,
     head_new,
     state_new,
+    chosen,
+    neg_t,
+    negs,
+    query,
+    rel_all,
     prob,
-    query,
     grad,
+    block_part,
     head_emb,
     head_grad,
     hot_head,
@@ -488,13 +408,21 @@
     deep_in,
     neg_total,
     slot_rows,
-    dense,
-    in_x,
-    in_y,
-    mid_x,
-    mid_y,
-    end_x,
-    end_y,
+    seats,
+    lo,
+    lo_in_x,
+    lo_in_y,
+    lo_mid_x,
+    lo_mid_y,
+    lo_end_x,
+    lo_end_y,
+    hi,
+    hi_in_x,
+    hi_in_y,
+    hi_mid_x,
+    hi_mid_y,
+    hi_end_x,
+    hi_end_y,
     update,
     sem_bs,
     sem_br,
@@ -504,8 +432,12 @@
     sem_pr,
     sem_zs,
     sem_zr,
-    sem_ds,
-    sem_dr,
+    sem_ls,
+    sem_lr,
+    sem_hs,
+    sem_hr,
+    sem_ns,
+    sem_nr,
     sem_us,
     sem_ur,
     sem_fs,
@@ -515,24 +447,24 @@
     head, tail = lax.axis_index("head"), lax.axis_index("tail")
     core, depth = lax.rem(head, 2), lax.div(head, 2)
     other = head + 1 - 2 * core
-    owned = own_t.shape[0]
-    width = own_t.shape[1]
+    owned, width, span = own_t.shape
     group = slots.shape[2]
     quarter = DEPTH // 2
+    blocks, edges = offsets.shape
+    half = width // 2
 
     def around(index, step, count):
         return lax.rem(index + step, count)
 
-    keep_block = pltpu.make_async_copy(block_part.at[head], slots.at[head], sem_local.at[0])
     loads = [
-        pltpu.make_async_copy(prob_hbm, prob, sem_local.at[1]),
-        pltpu.make_async_copy(query_hbm, query, sem_local.at[3]),
-        pltpu.make_async_copy(grad_hbm, grad, sem_local.at[4]),
-        pltpu.make_async_copy(head_hbm, head_emb, sem_local.at[5]),
+        pltpu.make_async_copy(neg_hbm, neg_t, sem_local.at[0]),
+        pltpu.make_async_copy(query_hbm, query, sem_local.at[1]),
+        pltpu.make_async_copy(chosen_hbm, chosen, sem_local.at[2]),
+        pltpu.make_async_copy(rel_hbm, rel_all, sem_local.at[3]),
+        pltpu.make_async_copy(head_hbm, head_emb, sem_local.at[4]),
     ]
     for load in loads:
         load.start()
-    keep_block.start()
 
     barrier = pltpu.get_barrier_semaphore()
 
@@ -546,8 +478,93 @@
         )
 
     loads[0].wait()
-    loads[1].wait()
-    blocks = prob.shape[0]
+    for k in range(negs.shape[0] // span):
+        negs[k * span : (k + 1) * span, :] = neg_t[:, k * span : (k + 1) * span].T
+    for load in loads[1:]:
+        load.wait()
+
+    def edge_block(b):
+        live = jnp.where(b < live_count[0], 1.0, 0.0).astype(F32)
+        pick = one_hot(span, offsets[pl.ds(b, 1), :])
+        tail_vec = mm(chosen[b], pick)
+        queries = query[b].astype(F32)
+        positive = jnp.sum(queries * tail_vec, axis=0, keepdims=True)
+        score = mm(negs[...], query[b])
+        largest = jnp.maximum(positive, jnp.max(score, axis=0, keepdims=True))
+        pos_exp = jnp.exp(positive - largest)
+        neg_exp = jnp.exp(score - largest)
+        denominator = pos_exp + jnp.sum(neg_exp, axis=0, keepdims=True)
+        pos_grad = (pos_exp / denominator - 1.0) * live
+        part = pos_grad * queries
+        part_a = part.astype(BF16)
+        rest = part - part_a.astype(F32)
+        part_b = rest.astype(BF16)
+        part_c = (rest - part_b.astype(F32)).astype(BF16)
+        block_grad = mm(pick, part_a, NT) + (mm(pick, part_b, NT) + mm(pick, part_c, NT))
+        number = (owners[b] * owned + locals_[b]).astype(F32)
+        for i in range(HEAD):
+            block_part[i, b, :, :width] = block_grad[i * group : (i + 1) * group].astype(BF16)
+            block_part[i, b, :, width:] = jnp.full((group, LANES - width), number, BF16)
+        prob[b] = (neg_exp * (live / denominator)).astype(BF16)
+        query_grad = pos_grad * tail_vec + mm(neg_t[...], prob[b])
+        rel = rel_all[b].astype(F32)
+        rr, ri = rel[:half], rel[half:]
+        qr, qi = query_grad[:half], query_grad[half:]
+        for start, change in ((0, qr * rr + qi * ri), (half, qi * rr - qr * ri)):
+            change_hi = change.astype(BF16)
+            grad[b, 0, start : start + half, :] = change_hi
+            grad[b, 1, start : start + half, :] = (change - change_hi.astype(F32)).astype(BF16)
+
+    early = blocks // 2
+    pieces = (
+        (pl.ds(0, early), pl.ds(0, LANES)),
+        (pl.ds(early, blocks - early), pl.ds(CUT, LANES - CUT)),
+        (pl.ds(early, blocks - early), pl.ds(0, CUT)),
+    )
+
+    def block_copy(piece, step):
+        which, lanes = pieces[piece]
+        peer = around(head, step, HEAD)
+        return remote(
+            block_part.at[peer, which, :, lanes],
+            slots.at[head, which, :, lanes],
+            sem_bs.at[piece, step],
+            sem_br.at[piece, step],
+            (peer, tail),
+        )
+
+    @pl.loop(0, early)
+    def _(b):
+        edge_block(b)
+
+    pl.semaphore_wait(barrier, HEAD + TAIL - 2)
+
+    @pl.loop(1, HEAD)
+    def _(step):
+        block_copy(0, step).start()
+
+    @pl.loop(early, blocks)
+    def _(b):
+        edge_block(b)
+
+    for piece in (1, 2):
+
+        @pl.loop(1, HEAD)
+        def _(step):
+            block_copy(piece, step).start()
+
+    keep_block = pltpu.make_async_copy(block_part.at[head], slots.at[head], sem_local.at[5])
+    keep_block.start()
+
+    def pair_copy(part):
+        return remote(
+            neg_part.at[part, :, :, 1 - core],
+            theirs.at[part],
+            sem_cs.at[part],
+            sem_cr.at[part],
+            (other, tail),
+        )
+
     chunk = prob.shape[1] // SIDE
 
     @pl.loop(0, SIDE)
@@ -557,30 +574,7 @@
         for b in range(1, blocks):
             total = total + mm(prob[b, spots, :], query[b], NT)
         neg_part[part] = total.reshape(neg_part.shape[1:])
-
-    pl.semaphore_wait(barrier, HEAD + TAIL - 2)
-
-    def pair_copy(part):
-        return remote(
-            neg_part.at[part, :, :, 1 - core],
-            theirs.at[part],
-            sem_cs.at[part],
-            sem_cr.at[part],
-            (other, tail),
-        )
-
-    for part in range(SIDE):
         pair_copy(part).start()
-
-    def block_copy(step):
-        peer = around(head, step, HEAD)
-        return remote(
-            block_part.at[peer], slots.at[head], sem_bs.at[step], sem_br.at[step], (peer, tail)
-        )
-
-    @pl.loop(1, HEAD)
-    def _(step):
-        block_copy(step).start()
 
     for part in range(SIDE):
         pair_copy(part).wait_recv()
@@ -591,16 +585,49 @@
     )
     plane.start_first()
 
-    loads[2].wait()
-    loads[3].wait()
-    rows, edges = hot_head.shape[0], head_rows.shape[1]
-    piece = 160
+    def spread_rows(piece):
+        which, lanes = pieces[piece]
+
+        @pl.loop(0, HEAD)
+        def _(source):
+            for b in range(which.start, which.start + which.size):
+                spot = pl.multiple_of((source * owned + b) * group, group)
+                slot_rows[pl.ds(spot, group), lanes] = slots[source, b, :, lanes].astype(F32)
+
+    def arrive(piece):
+        @pl.loop(1, HEAD)
+        def _(step):
+            block_copy(piece, step).wait_recv()
+
+        if piece == 0:
+            keep_block.wait()
+        spread_rows(piece)
+
+    def fill(dense, sums):
+        for block in range(TAIL * owned):
+            y, x, part = block // owned // SIDE, block // owned % SIDE, block % owned
+            dense[y, x, part] = sums[block * group : (block + 1) * group]
+
+    arrive(0)
+    arrive(1)
+    count = HEAD * owned * group
+    number = slot_rows[:, width : width + 1]
+    inner = lax.broadcasted_iota(jnp.int32, (count, 1), 0) % group
+    goal = number * group + inner.astype(F32)
+    places = lax.broadcasted_iota(jnp.int32, (count, count), 1).astype(F32)
+    seats[...] = jnp.where(places == goal, 1.0, 0.0).astype(BF16).T
+    fill(hi, mm(seats[...], slot_rows[:, CUT:width].astype(BF16)))
+    high = PlaneSum(hi, hi_in_x, hi_in_y, hi_mid_x, hi_mid_y, hi_end_x, hi_end_y, (sem_hs, sem_hr))
+    high.start_first()
+
+    rows = hot_head.shape[0]
+    piece_rows = 160
     for b in range(blocks):
         hot_head[:, b * edges : (b + 1) * edges] = one_hot(rows, head_rows[b : b + 1, :])
 
     def head_piece(p, squares):
-        spots = pl.ds(pl.multiple_of(p * piece, piece), piece)
-        gradient = jnp.zeros((piece, rows), F32)
+        spots = pl.ds(pl.multiple_of(p * piece_rows, piece_rows), piece_rows)
+        gradient = jnp.zeros((piece_rows, rows), F32)
         for b in range(blocks):
             lanes = slice(b * edges, (b + 1) * edges)
             for n in range(2):
@@ -608,26 +635,35 @@
         head_grad[spots, :] = gradient
         return squares + jnp.sum(gradient * gradient, axis=0, keepdims=True)
 
-    squares = lax.fori_loop(0, width // piece, head_piece, jnp.zeros((1, rows), F32))
+    squares = lax.fori_loop(0, width // piece_rows, head_piece, jnp.zeros((1, rows), F32))
+
+    arrive(2)
+    fill(lo, mm(seats[...], slot_rows[:, :CUT].astype(BF16)))
+    low = PlaneSum(lo, lo_in_x, lo_in_y, lo_mid_x, lo_mid_y, lo_end_x, lo_end_y, (sem_ls, sem_lr))
+    low.start_first()
     plane.start_second()
+    high.start_second()
+
     head_next = head_state[...] + squares / width
     state_new[...] = head_next
     rate = LEARN_RATE / jnp.sqrt(head_next)
 
-    @pl.loop(0, width // piece)
+    @pl.loop(0, width // piece_rows)
     def _(p):
-        spots = pl.ds(pl.multiple_of(p * piece, piece), piece)
+        spots = pl.ds(pl.multiple_of(p * piece_rows, piece_rows), piece_rows)
         head_emb[spots, :] = (head_emb[spots, :].astype(F32) - head_grad[spots, :] * rate).astype(
             BF16
         )
 
     head_store = pltpu.make_async_copy(head_emb, head_new, sem_local.at[6])
     head_store.start()
+
     for place, total in enumerate(plane.result()):
         deep[place] = total
 
     zone = lax.rem(tail, 2)
     takes = lax.div(depth, quarter) == zone
+    mine_k = lax.div(tail, 2)
 
     def deep_copy(step):
         level = zone * quarter + step
@@ -644,33 +680,32 @@
             deep.at[0], deep_in.at[source], sem_zs.at[0], sem_zr.at[source], (other, tail)
         )
 
+    def total_copy(step):
+        return remote(
+            neg_total.at[mine_k],
+            neg_total.at[mine_k],
+            sem_ns.at[step],
+            sem_nr.at[mine_k],
+            (head, around(tail, step, TAIL)),
+        )
+
+    def total_landing(k):
+        return remote(neg_total.at[k], neg_total.at[k], sem_ns.at[1], sem_nr.at[k], (other, tail))
+
     @pl.loop(0, quarter)
     def _(step):
         @pl.when(zone * quarter + step != depth)
         def _():
             deep_copy(step).start()
 
-    neg_total[...] = jnp.zeros_like(neg_total)
-
-    keep_block.wait()
-
-    @pl.loop(1, HEAD)
-    def _(step):
-        block_copy(step).wait_recv()
-
-    @pl.loop(0, HEAD)
-    def _(source):
-        for b in range(owned):
-            spot = pl.multiple_of((source * owned + b) * group, group)
-            slot_rows[pl.ds(spot, group), :] = slots[source, b].astype(F32)
-
-    count = HEAD * owned * group
-    number = slot_rows[:, width : width + 1]
-    inner = lax.broadcasted_iota(jnp.int32, (count, 1), 0) % group
-    goal = number * group + inner.astype(F32)
-    spots = lax.broadcasted_iota(jnp.int32, (count, count), 1).astype(F32)
-    hot = jnp.where(spots == goal, 1.0, 0.0).astype(BF16)
-    sums = mm(hot, slot_rows[:, :width].astype(BF16), TN)
+    low.start_second()
+    lane = lax.broadcasted_iota(jnp.int32, (group, span), 1)
+    mark = lane == head * group + lax.broadcasted_iota(jnp.int32, (group, span), 0)
+    rows_now = [mm(jnp.where(mark, 1.0, 0.0).astype(BF16), own_t[b], NT) for b in range(owned)]
+    states_now = [
+        jnp.sum(jnp.where(mark, own_state[b : b + 1, :], 0.0), axis=1, keepdims=True)
+        for b in range(owned)
+    ]
 
     @pl.when(takes)
     def _():
@@ -685,39 +720,39 @@
         total = deep_in[0]
         for source in range(1, DEPTH):
             total = total + deep_in[source]
-        neg_total[...] = total
-
-    target = neg_ids[lax.div(tail, 2)]
-    total = neg_total[...]
-    for block in range(TAIL * owned):
-        y, x, part = block // owned // SIDE, block // owned % SIDE, block % owned
-        weight = jnp.where(target == block, 1.0, 0.0).astype(F32)
-        dense[y, x, part] = sums[block * group : (block + 1) * group] + weight * total
-
-    table = PlaneSum(dense, in_x, in_y, mid_x, mid_y, end_x, end_y, (sem_ds, sem_dr))
-    table.start_first()
-    lane = lax.broadcasted_iota(jnp.int32, (group, own_t.shape[2]), 1)
-    mark = lane == head * group + lax.broadcasted_iota(jnp.int32, (group, own_t.shape[2]), 0)
-    rows_now = [
-        mm(jnp.where(mark, 1.0, 0.0).astype(BF16), own_t[b], NT) for b in range(owned)
-    ]
-    states_now = [
-        jnp.sum(jnp.where(mark, own_state[b : b + 1, :], 0.0), axis=1, keepdims=True)
-        for b in range(owned)
-    ]
-    table.start_second()
-
-    for b, gradient in enumerate(table.result()):
-        fresh = states_now[b] + jnp.sum(gradient * gradient, axis=1, keepdims=True) / width
-        update[b, :, :width] = (
-            rows_now[b] - gradient * (LEARN_RATE / jnp.sqrt(fresh))
-        ).astype(BF16)
+        neg_total[mine_k] = total
+
+        @pl.loop(1, TAIL)
+        def _(step):
+            total_copy(step).start()
+
+    high_sums, low_sums = high.result(), low.result()
+
+    @pl.loop(0, neg_total.shape[0])
+    def _(k):
+        @pl.when(2 * k + lax.div(depth, quarter) != tail)
+        def _():
+            total_landing(k).wait_recv()
+
+    for b in range(owned):
+        low_part, high_part = low_sums[b], high_sums[b]
+        for k in range(neg_total.shape[0]):
+            weight = jnp.where(neg_ids[k] == tail * owned + b, 1.0, 0.0).astype(F32)
+            low_part = low_part + weight * neg_total[k, :, :CUT]
+            high_part = high_part + weight * neg_total[k, :, CUT:]
+        squares = jnp.sum(low_part * low_part, axis=1, keepdims=True) + jnp.sum(
+            high_part * high_part, axis=1, keepdims=True
+        )
+        fresh = states_now[b] + squares / width
+        rate = LEARN_RATE / jnp.sqrt(fresh)
+        update[b, :, :CUT] = (rows_now[b][:, :CUT] - low_part * rate).astype(BF16)
+        update[b, :, CUT:width] = (rows_now[b][:, CUT:] - high_part * rate).astype(BF16)
         spot = lax.broadcasted_iota(jnp.int32, (group, LANES - width), 1)
         fresh_a = fresh.astype(BF16).astype(F32)
         fresh_b = (fresh - fresh_a).astype(BF16).astype(F32)
         fresh_c = fresh - fresh_a - fresh_b
-        pieces = jnp.where(spot == 0, fresh_a, jnp.where(spot == 1, fresh_b, fresh_c))
-        update[b, :, width:] = pieces.astype(BF16)
+        parts = jnp.where(spot == 0, fresh_a, jnp.where(spot == 1, fresh_b, fresh_c))
+        update[b, :, width:] = parts.astype(BF16)
 
     def rows_copy(step):
         peer = around(depth, step, DEPTH) * 2 + core
@@ -727,7 +762,7 @@
     def _(step):
         rows_copy(step).start()
 
-    out_own = pltpu.make_async_copy(update, out.at[:, head], sem_local.at[2])
+    out_own = pltpu.make_async_copy(update, out.at[:, head], sem_local.at[7])
     out_own.start()
     first_rows = remote(update, out.at[:, head], sem_fs.at[0], sem_fr.at[0], (other, tail))
     first_rows.start()
@@ -738,19 +773,17 @@
             out.at[:, place], out.at[:, place], sem_fs.at[step], sem_fr.at[step], (other, tail)
         )
 
-    @pl.loop(1, DEPTH)
-    def _(step):
-        rows_copy(step).wait_recv()
-        pass_rows(step).start()
-
     plane.finish()
-    table.finish()
+    high.finish()
+    low.finish()
     for part in range(SIDE):
         pair_copy(part).wait_send()
 
-    @pl.loop(1, HEAD)
-    def _(step):
-        block_copy(step).wait_send()
+    for piece in range(3):
+
+        @pl.loop(1, HEAD)
+        def _(step):
+            block_copy(piece, step).wait_send()
 
     @pl.loop(0, quarter)
     def _(step):
@@ -758,8 +791,20 @@
         def _():
             deep_copy(step).wait_send()
 
+    @pl.when(takes)
+    def _():
+        @pl.loop(1, TAIL)
+        def _(step):
+            total_copy(step).wait_send()
+
+    head_store.wait()
+
+    @pl.loop(1, DEPTH)
+    def _(step):
+        rows_copy(step).wait_recv()
+        pass_rows(step).start()
+
     out_own.wait()
-    head_store.wait()
     first_rows.wait()
 
     @pl.loop(1, DEPTH)
@@ -769,22 +814,41 @@
 
 
 def run_exchange(
-    neg_ids, block_part, prob, query, grad, head_t, head_rows, head_state, own_t, own_state
+    owners,
+    locals_,
+    live_count,
+    neg_ids,
+    chosen,
+    neg_t,
+    query,
+    rel_vec,
+    head_t,
+    offsets,
+    head_rows,
+    head_state,
+    own_t,
+    own_state,
 ):
+    owned, width, span = own_t.shape
+    blocks, edges = offsets.shape
     rows = head_t.shape[1]
-    total = head_rows.shape[0] * head_rows.shape[1]
-    owned, width, span = own_t.shape
     group = span // HEAD
+    negs = neg_ids.shape[0]
     quarter = DEPTH // 2
+    count = HEAD * owned * group
     sems = pltpu.SemaphoreType.DMA
+    smem = pl.BlockSpec(memory_space=pltpu.SMEM)
     anywhere = pl.BlockSpec(memory_space=pl.ANY)
     vmem = pl.BlockSpec(memory_space=pltpu.VMEM)
-    whole = pltpu.VMEM((SIDE, SIDE, 4, group, width), F32)
-    plane_sum = (
-        [pltpu.VMEM((SIDE - 1, SIDE, 2, group, width), F32)] * 2
-        + [pltpu.VMEM((SIDE, 2, group, width), F32)] * 2
-        + [pltpu.VMEM((SIDE - 1, 2, group, width), F32)] * 2
-    )
+
+    def plane_sum(columns):
+        return [
+            pltpu.VMEM((SIDE, SIDE, 4, group, columns), F32),
+            *([pltpu.VMEM((SIDE - 1, SIDE, 2, group, columns), F32)] * 2),
+            *([pltpu.VMEM((SIDE, 2, group, columns), F32)] * 2),
+            *([pltpu.VMEM((SIDE - 1, 2, group, columns), F32)] * 2),
+        ]
+
     return pl.pallas_call(
         exchange,
         out_shape=(
@@ -792,32 +856,34 @@
             jax.ShapeDtypeStruct(head_t.shape, BF16),
             jax.ShapeDtypeStruct((1, rows), F32),
         ),
-        in_specs=[pl.BlockSpec(memory_space=pltpu.SMEM)]
-        + [anywhere] * 4
-        + [pl.BlockSpec(memory_space=pltpu.HBM)]
-        + [vmem] * 4,
+        in_specs=[smem] * 4 + [anywhere] * 5 + [vmem] * 5,
         out_specs=(anywhere, anywhere, vmem),
         scratch_shapes=[
-            pltpu.VMEM(prob.shape, BF16),
+            pltpu.VMEM(chosen.shape, BF16),
+            pltpu.VMEM(neg_t.shape, BF16),
+            pltpu.VMEM((negs * span, width), BF16),
             pltpu.VMEM(query.shape, BF16),
-            pltpu.VMEM(grad.shape, BF16),
+            pltpu.VMEM(rel_vec.shape, BF16),
+            pltpu.VMEM((blocks, negs * span, edges), BF16),
+            pltpu.VMEM((blocks, 2, width, edges), BF16),
+            pltpu.VMEM((HEAD, blocks, group, LANES), BF16),
             pltpu.VMEM(head_t.shape, BF16),
             pltpu.VMEM(head_t.shape, F32),
-            pltpu.VMEM((rows, total), BF16),
+            pltpu.VMEM((rows, blocks * edges), BF16),
             pltpu.VMEM((SIDE, SIDE, 4, 2, group, width), F32),
             pltpu.VMEM((HEAD, owned, group, LANES), BF16),
-            whole,
-            whole,
-            *plane_sum,
+            pltpu.VMEM((SIDE, SIDE, 4, group, width), F32),
+            *plane_sum(width),
             pltpu.VMEM((quarter, group, width), F32),
             pltpu.VMEM((DEPTH, group, width), F32),
-            pltpu.VMEM((group, width), F32),
-            pltpu.VMEM((HEAD * owned * group, LANES), F32),
-            whole,
-            *plane_sum,
+            pltpu.VMEM((negs, group, width), F32),
+            pltpu.VMEM((count, LANES), F32),
+            pltpu.VMEM((count, count), BF16),
+            *plane_sum(CUT),
+            *plane_sum(width - CUT),
             pltpu.VMEM((owned, group, LANES), BF16),
-            sems((HEAD,)),
-            sems((HEAD,)),
+            sems((3, HEAD)),
+            sems((3, HEAD)),
             sems((SIDE,)),
             sems((SIDE,)),
             sems((12,)),
@@ -826,16 +892,35 @@
             sems((DEPTH,)),
             sems((12,)),
             sems((12,)),
+            sems((12,)),
+            sems((12,)),
+            sems((TAIL,)),
+            sems((negs,)),
             sems((DEPTH,)),
             sems((DEPTH,)),
             sems((DEPTH,)),
             sems((DEPTH,)),
-            sems((7,)),
+            sems((8,)),
         ],
         compiler_params=pltpu.CompilerParams(
             collective_id=1, has_side_effects=True, vmem_limit_bytes=VMEM_BYTES
         ),
-    )(neg_ids, block_part, prob, query, grad, head_t, head_rows, head_state, own_t, own_state)
+    )(
+        owners,
+        locals_,
+        live_count,
+        neg_ids,
+        chosen,
+        neg_t,
+        query,
+        rel_vec,
+        head_t,
+        offsets,
+        head_rows,
+        head_state,
+        own_t,
+        own_state,
+    )
 
 
 def per_device(
@@ -855,23 +940,21 @@
     owned, span, width = tail_emb.shape
     head_t, tail_t = head_emb.T, tail_emb.transpose(0, 2, 1)
     table, query, rel_vec = gather_table(tail_t, head_t, relation_emb.T, head_rows, relations)
-    block_part, prob, grad = run_edges(
-        tail_owner.reshape(-1),
+    owners = tail_owner.reshape(-1)
+    chosen, neg_t = run_pick(
+        owners, tail_local, neg_blocks, table.reshape(TAIL * owned, width, span)
+    )
+    fresh, head_new, head_state_new = run_exchange(
+        owners,
         tail_local,
+        block_count,
         neg_blocks,
-        block_count,
-        table.reshape(TAIL * owned, width, span),
+        chosen,
+        neg_t,
         query,
         rel_vec,
+        head_t,
         tail_offsets,
-    )
-    fresh, head_new, head_state_new = run_exchange(
-        neg_blocks,
-        block_part,
-        prob,
-        query,
-        grad,
-        head_t,
         head_rows,
         head_state[None, :],
         tail_t,

time: 139 us -> 211 us (1.52)
  Pallas kernels: 132 us -> 204 us
    pallas_call x1, Pallas kernels: 17.6 us -> 76.3 us  [run_pick(): pl.pallas_call(pick_blocks, out_shape=(jax.ShapeDtypeStruct((blocks, widt...]
    pallas_call x1, Pallas kernels: 69.6 us -> 82.1 us  [run_exchange(): pl.pallas_call(exchange, out_shape=(jax.ShapeDtypeStruct((owned, HEAD, gr...]
where the time goes in v4:
time: 211 us; the launch traced here: 210 us
  Pallas kernels  204 us (97%)
  local copies, waits for them, and re-layouts  4.86 us (2%)
    pallas_call x1, Pallas kernels, run_exchange(): pl.pallas_call(exchange, out_shape=(jax.ShapeDtypeStruct((owned, HEAD, gr...  82.1 us
    pallas_call x1, Pallas kernels, run_pick(): pl.pallas_call(pick_blocks, out_shape=(jax.ShapeDtypeStruct((blocks, widt...  76.3 us
    pallas_call x1, Pallas kernels, gather_table(): pl.pallas_call(table_gather, out_shape=(jax.ShapeDtypeStruct((TAIL,) + ta...  45.1 us

profile of v4, /device:TPU:1, one launch (start us, length us, event | category | flops | bytes accessed | tf_op | source)
XLA Modules:
  0.0 210.4 jit_solution(1002389805915350960)
XLA Ops:
  0.6 45.1 %shard_map.147 = (bf16[16,4,800,128]{3,2,1,0:T(8,128)(2,1)}, bf16[4,800,256]{2,1,0:T(8,128)(2,1)}, bf16[4,800,256]{2,1,0:T(8,128)(2,1)}) custom-call(bf16[4,800,128]{2,1,0:T(8,128)(2,1)} %bitcast.13, bf16[800,512]{1,0:T(8,128)(2,1)} %bitcast.15, bf16[800,1024]{1,0:T(8,128)(2,1)} %bitcast.17, s32[4,256]{1,0:T(4,128)} %head_rows.1, s32[4,256]{1,0:T(4,128)} %relations_hbm.1), custom_call_target="tpu_custom_call" | custom-call | tf_op jit(solution)/shard_map/pallas_call | solution.py:210
  45.8 76.3 %shard_map.148 = (bf16[4,800,128]{2,1,0:T(8,128)(2,1)}, bf16[800,1024]{1,0:T(8,128)(2,1)}) custom-call(s32[4]{0:T(128)} %bitcast.22, s32[4]{0:T(128)} %locals_.3, s32[8]{0:T(128)} %neg_ids.3, bf16[64,800,128]{2,1,0:T(8,128)(2,1)} %bitcast.12), custom_call_target="tpu_custom_call" | custom-call | tf_op jit(solution)/shard_map/pallas_call | solution.py:262
  122.8 82.1 %shard_map.149 = (bf16[4,16,8,896]{3,2,1,0:T(8,128)(2,1)}, bf16[800,512]{1,0:T(8,128)(2,1)}, f32[1,512]{1,0:T(1,128)}) custom-call(s32[4]{0:T(128)} %bitcast.23, s32[4]{0:T(128)} %locals_.3, s32[1]{0:T(128)S(6)} %copy.22.live_count, s32[8]{0:T(128)} %neg_ids.3, bf16[4,800,128]{2,1,0:T(8,128)(2,1)} %get-tuple-element.13.chosen_hbm, ...), custom_call_target="tpu_custom_call" | custom-call | tf_op jit(solution)/shard_map/pallas_call | solution.py:852
  204.9 0.0 copy-start
  204.9 0.0 copy-start.1
  204.9 2.3 %copy.18 = bf16[4,128,800]{1,2,0:T(8,128)(2,1)} copy(bf16[4,128,800]{2,1,0:T(8,128)(2,1)} %bitcast.18) | data formatting | bytes 1638400
  207.2 1.0 slice.21
  208.2 0.1 copy.19
  208.3 0.6 fusion
  208.9 0.0 copy-done
  208.9 0.9 copy.23
  209.8 0.0 copy-done.1
  209.8 0.6 copy.24
  (1 shorter events, 0.0 us)
Async XLA Ops:
  204.9 4.0 %copy-start = (bf16[800,512]{1,0:T(8,128)(2,1)S(1)}, bf16[800,512]{1,0:T(8,128)(2,1)}, u32[]{:S(2)}) copy-start(bf16[800,512]{1,0:T(8,128)(2,1)} %get-tuple-element.17) | copy-start | bytes 2457604
  204.9 4.9 %copy-start.1 = (f32[1,512]{1,0:T(1,128)S(1)}, f32[1,512]{1,0:T(1,128)}, u32[]{:S(2)}) copy-start(f32[1,512]{1,0:T(1,128)} %get-tuple-element.18) | copy-start | bytes 6148

commit v5 on v4

--- a/solution.py
+++ b/solution.py
@@ -258,6 +258,7 @@
     blocks, negs = owners.shape[0], neg_ids.shape[0]
     width, span = table.shape[1:]
     smem = pl.BlockSpec(memory_space=pltpu.SMEM)
+    vmem = pl.BlockSpec(memory_space=pltpu.VMEM)
     anywhere = pl.BlockSpec(memory_space=pl.ANY)
     return pl.pallas_call(
         pick_blocks,
@@ -266,7 +267,7 @@
             jax.ShapeDtypeStruct((width, negs * span), BF16),
         ),
         in_specs=[smem, smem, smem, anywhere],
-        out_specs=(anywhere, anywhere),
+        out_specs=(vmem, vmem),
         scratch_shapes=[pltpu.SemaphoreType.DMA((blocks + negs,))],
         compiler_params=pltpu.CompilerParams(vmem_limit_bytes=VMEM_BYTES),
     )(owners, locals_, neg_ids, table)
@@ -619,6 +620,7 @@
     fill(hi, mm(seats[...], slot_rows[:, CUT:width].astype(BF16)))
     high = PlaneSum(hi, hi_in_x, hi_in_y, hi_mid_x, hi_mid_y, hi_end_x, hi_end_y, (sem_hs, sem_hr))
     high.start_first()
+    plane.start_second()
 
     rows = hot_head.shape[0]
     piece_rows = 160
@@ -637,27 +639,6 @@
 
     squares = lax.fori_loop(0, width // piece_rows, head_piece, jnp.zeros((1, rows), F32))
 
-    arrive(2)
-    fill(lo, mm(seats[...], slot_rows[:, :CUT].astype(BF16)))
-    low = PlaneSum(lo, lo_in_x, lo_in_y, lo_mid_x, lo_mid_y, lo_end_x, lo_end_y, (sem_ls, sem_lr))
-    low.start_first()
-    plane.start_second()
-    high.start_second()
-
-    head_next = head_state[...] + squares / width
-    state_new[...] = head_next
-    rate = LEARN_RATE / jnp.sqrt(head_next)
-
-    @pl.loop(0, width // piece_rows)
-    def _(p):
-        spots = pl.ds(pl.multiple_of(p * piece_rows, piece_rows), piece_rows)
-        head_emb[spots, :] = (head_emb[spots, :].astype(F32) - head_grad[spots, :] * rate).astype(
-            BF16
-        )
-
-    head_store = pltpu.make_async_copy(head_emb, head_new, sem_local.at[6])
-    head_store.start()
-
     for place, total in enumerate(plane.result()):
         deep[place] = total
 
@@ -698,7 +679,45 @@
         def _():
             deep_copy(step).start()
 
-    low.start_second()
+    arrive(2)
+    fill(lo, mm(seats[...], slot_rows[:, :CUT].astype(BF16)))
+    low = PlaneSum(lo, lo_in_x, lo_in_y, lo_mid_x, lo_mid_y, lo_end_x, lo_end_y, (sem_ls, sem_lr))
+    low.start_first()
+    @pl.when(takes)
+    def _():
+        deep_in[depth] = deep[depth - zone * quarter]
+
+        @pl.loop(0, DEPTH)
+        def _(source):
+            @pl.when(source != depth)
+            def _():
+                deep_landing(source).wait_recv()
+
+        total = deep_in[0]
+        for source in range(1, DEPTH):
+            total = total + deep_in[source]
+        neg_total[mine_k] = total
+
+        @pl.loop(1, TAIL)
+        def _(step):
+            total_copy(step).start()
+
+    high.start_second()
+
+    head_next = head_state[...] + squares / width
+    state_new[...] = head_next
+    rate = LEARN_RATE / jnp.sqrt(head_next)
+
+    @pl.loop(0, width // piece_rows)
+    def _(p):
+        spots = pl.ds(pl.multiple_of(p * piece_rows, piece_rows), piece_rows)
+        head_emb[spots, :] = (head_emb[spots, :].astype(F32) - head_grad[spots, :] * rate).astype(
+            BF16
+        )
+
+    head_store = pltpu.make_async_copy(head_emb, head_new, sem_local.at[6])
+    head_store.start()
+
     lane = lax.broadcasted_iota(jnp.int32, (group, span), 1)
     mark = lane == head * group + lax.broadcasted_iota(jnp.int32, (group, span), 0)
     rows_now = [mm(jnp.where(mark, 1.0, 0.0).astype(BF16), own_t[b], NT) for b in range(owned)]
@@ -707,25 +726,7 @@
         for b in range(owned)
     ]
 
-    @pl.when(takes)
-    def _():
-        deep_in[depth] = deep[depth - zone * quarter]
-
-        @pl.loop(0, DEPTH)
-        def _(source):
-            @pl.when(source != depth)
-            def _():
-                deep_landing(source).wait_recv()
-
-        total = deep_in[0]
-        for source in range(1, DEPTH):
-            total = total + deep_in[source]
-        neg_total[mine_k] = total
-
-        @pl.loop(1, TAIL)
-        def _(step):
-            total_copy(step).start()
-
+    low.start_second()
     high_sums, low_sums = high.result(), low.result()
 
     @pl.loop(0, neg_total.shape[0])

time: 211 us -> 134 us (0.64)
  Pallas kernels: 204 us -> 127 us
    pallas_call x1, Pallas kernels: 76.3 us -> 3.97 us  [run_pick(): pl.pallas_call(pick_blocks, out_shape=(jax.ShapeDtypeStruct((blocks, widt...]
    pallas_call x1, Pallas kernels: 82.1 us -> 77.5 us  [run_exchange(): pl.pallas_call(exchange, out_shape=(jax.ShapeDtypeStruct((owned, HEAD, gr...]
where the time goes in v5:
time: 134 us; the launch traced here: 133 us
  Pallas kernels  127 us (95%)
  local copies, waits for them, and re-layouts  4.86 us (4%)
    pallas_call x1, Pallas kernels, run_exchange(): pl.pallas_call(exchange, out_shape=(jax.ShapeDtypeStruct((owned, HEAD, gr...  77.5 us
    pallas_call x1, Pallas kernels, gather_table(): pl.pallas_call(table_gather, out_shape=(jax.ShapeDtypeStruct((TAIL,) + ta...  45.1 us
    pallas_call x1, Pallas kernels, run_pick(): pl.pallas_call(pick_blocks, out_shape=(jax.ShapeDtypeStruct((blocks, widt...  3.97 us
    unnamed x8, local copies, waits for them, and re-layouts  3.85 us

profile of v5, /device:TPU:1, one launch (start us, length us, event | category | flops | bytes accessed | tf_op | source)
XLA Modules:
  0.0 133.3 jit_solution(7659253814076361093)
XLA Ops:
  0.6 45.1 %shard_map.147 = (bf16[16,4,800,128]{3,2,1,0:T(8,128)(2,1)}, bf16[4,800,256]{2,1,0:T(8,128)(2,1)}, bf16[4,800,256]{2,1,0:T(8,128)(2,1)}) custom-call(bf16[4,800,128]{2,1,0:T(8,128)(2,1)} %bitcast.13, bf16[800,512]{1,0:T(8,128)(2,1)} %bitcast.15, bf16[800,1024]{1,0:T(8,128)(2,1)} %bitcast.17, s32[4,256]{1,0:T(4,128)} %head_rows.1, s32[4,256]{1,0:T(4,128)} %relations_hbm.1), custom_call_target="tpu_custom_call" | custom-call | tf_op jit(solution)/shard_map/pallas_call | solution.py:210
  45.8 4.0 %shard_map.148 = (bf16[4,800,128]{2,1,0:T(8,128)(2,1)}, bf16[800,1024]{1,0:T(8,128)(2,1)}) custom-call(s32[4]{0:T(128)} %bitcast.22, s32[4]{0:T(128)} %locals_.3, s32[8]{0:T(128)} %neg_ids.3, bf16[64,800,128]{2,1,0:T(8,128)(2,1)} %bitcast.12), custom_call_target="tpu_custom_call" | custom-call | tf_op jit(solution)/shard_map/pallas_call | solution.py:263
  50.4 77.5 %shard_map.149 = (bf16[4,16,8,896]{3,2,1,0:T(8,128)(2,1)}, bf16[800,512]{1,0:T(8,128)(2,1)}, f32[1,512]{1,0:T(1,128)}) custom-call(s32[4]{0:T(128)} %bitcast.23, s32[4]{0:T(128)} %locals_.3, s32[1]{0:T(128)S(6)} %copy.22.live_count, s32[8]{0:T(128)} %neg_ids.3, bf16[4,800,128]{2,1,0:T(8,128)(2,1)} %get-tuple-element.13.chosen_hbm, ...), custom_call_target="tpu_custom_call" | custom-call | tf_op jit(solution)/shard_map/pallas_call | solution.py:853
  127.8 0.0 copy-start
  127.9 0.0 copy-start.1
  127.9 2.3 %copy.18 = bf16[4,128,800]{1,2,0:T(8,128)(2,1)} copy(bf16[4,128,800]{2,1,0:T(8,128)(2,1)} %bitcast.18) | data formatting | bytes 1638400
  130.1 1.0 slice.21
  131.1 0.1 copy.19
  131.3 0.6 fusion
  131.9 0.0 copy-done
  131.9 0.9 copy.23
  132.8 0.0 copy-done.1
  132.8 0.6 copy.24
  (1 shorter events, 0.0 us)
Async XLA Ops:
  127.8 4.0 %copy-start = (bf16[800,512]{1,0:T(8,128)(2,1)S(1)}, bf16[800,512]{1,0:T(8,128)(2,1)}, u32[]{:S(2)}) copy-start(bf16[800,512]{1,0:T(8,128)(2,1)} %get-tuple-element.17) | copy-start | bytes 2457604
  127.9 4.9 %copy-start.1 = (f32[1,512]{1,0:T(1,128)S(1)}, f32[1,512]{1,0:T(1,128)}, u32[]{:S(2)}) copy-start(f32[1,512]{1,0:T(1,128)} %get-tuple-element.18) | copy-start | bytes 6148

commit v6 on v5

--- a/solution.py
+++ b/solution.py
@@ -39,14 +39,21 @@
 
 
 def table_gather(
+    owners,
+    locals_,
+    neg_ids,
     own,
     head_hbm,
     rel_hbm,
     head_rows_hbm,
     relations_hbm,
-    table,
     query_out,
     rel_out,
+    chosen_out,
+    neg_out,
+    table,
+    chosen,
+    neg_t,
     head_t,
     rel_t,
     head_rows,
@@ -65,6 +72,7 @@
     core, col, row = lax.rem(head, 2), lax.rem(tail, SIDE), lax.div(tail, SIDE)
     sibling = (head + 1 - 2 * core, tail)
     size = own.shape[1]
+    owned, span = own.shape[0], own.shape[2]
     everything = (0, size)
     first, second = (0, size // 2), (size // 2, size // 2)
     blocks = query.shape[0]
@@ -72,7 +80,7 @@
     loads = [
         pltpu.make_async_copy(head_hbm, head_t, local.at[0]),
         pltpu.make_async_copy(rel_hbm, rel_t, local.at[1]),
-        pltpu.make_async_copy(own, table.at[tail], local.at[2]),
+        pltpu.make_async_copy(own, table.at[pl.ds(tail * owned, owned)], local.at[2]),
         pltpu.make_async_copy(head_rows_hbm, head_rows, local.at[3 + 2 * blocks]),
         pltpu.make_async_copy(relations_hbm, relations, local.at[4 + 2 * blocks]),
     ]
@@ -92,7 +100,7 @@
     def copy(which, origin, part, sems, spot, target):
         block = 2 * core + which
         start, count = part
-        here = table.at[place(which, *origin), block, pl.ds(start, count)]
+        here = table.at[place(which, *origin) * owned + block, pl.ds(start, count)]
         source = own.at[block, pl.ds(start, count)] if origin == (0, 0) else here
         return pltpu.make_async_remote_copy(
             src_ref=source,
@@ -106,7 +114,7 @@
     def landing(which, origin, part, sems, spot, block=None):
         block = 2 * core + which if block is None else block
         start, count = part
-        here = table.at[place(which, *origin), block, pl.ds(start, count)]
+        here = table.at[place(which, *origin) * owned + block, pl.ds(start, count)]
         return pltpu.make_async_remote_copy(
             src_ref=here,
             dst_ref=here,
@@ -196,13 +204,23 @@
                     spot = along * 4 + across
                     landing(which, (along, across), everything, stage3, spot, block).wait_recv()
     loads[2].wait()
+    for k in range(neg_ids.shape[0]):
+        neg_t[:, k * span : (k + 1) * span] = table[neg_ids[k]]
+    for b in range(blocks):
+        chosen[b] = table[owners[b] * owned + locals_[b]]
+    for n, (value, target) in enumerate(((neg_t, neg_out), (chosen, chosen_out))):
+        store = pltpu.make_async_copy(value, target, local.at[5 + 2 * blocks + n])
+        store.start()
+        stores.append(store)
     for store in stores:
         store.wait()
     for transfer in sent:
         transfer.wait_send()
 
 
-def gather_table(tail_t, head_t, rel_t, head_rows, relations):
+def gather_table(owners, locals_, neg_ids, tail_t, head_t, rel_t, head_rows, relations):
+    owned, _, span = tail_t.shape
+    negs = neg_ids.shape[0]
     blocks, edges = head_rows.shape
     width = head_t.shape[0]
     sems = pltpu.SemaphoreType.DMA
@@ -210,13 +228,18 @@
     return pl.pallas_call(
         table_gather,
         out_shape=(
-            jax.ShapeDtypeStruct((TAIL,) + tail_t.shape, BF16),
             jax.ShapeDtypeStruct((blocks, width, edges), BF16),
             jax.ShapeDtypeStruct((blocks, width, edges), BF16),
+            jax.ShapeDtypeStruct((blocks, width, span), BF16),
+            jax.ShapeDtypeStruct((width, negs * span), BF16),
         ),
-        in_specs=[pl.BlockSpec(memory_space=pltpu.HBM)] * 5,
-        out_specs=(anywhere, anywhere, anywhere),
+        in_specs=[pl.BlockSpec(memory_space=pltpu.SMEM)] * 3
+        + [pl.BlockSpec(memory_space=pltpu.HBM)] * 5,
+        out_specs=(anywhere, anywhere, anywhere, anywhere),
         scratch_shapes=[
+            pltpu.VMEM((TAIL * owned, width, span), BF16),
+            pltpu.VMEM((blocks, width, span), BF16),
+            pltpu.VMEM((width, negs * span), BF16),
             pltpu.VMEM(head_t.shape, BF16),
             pltpu.VMEM(rel_t.shape, BF16),
             pltpu.VMEM(head_rows.shape, jnp.int32),
@@ -229,48 +252,12 @@
             sems((2, 16)),
             sems((2, 16)),
             sems((2, 16)),
-            sems((5 + 2 * blocks,)),
+            sems((7 + 2 * blocks,)),
         ],
         compiler_params=pltpu.CompilerParams(
             collective_id=0, has_side_effects=True, vmem_limit_bytes=VMEM_BYTES
         ),
-    )(tail_t, head_t, rel_t, head_rows, relations)
-
-
-def pick_blocks(owners, locals_, neg_ids, table, chosen, neg_t, sems):
-    owned = table.shape[0] // TAIL
-    span = table.shape[2]
-    copies = []
-    for k in range(neg_ids.shape[0]):
-        lanes = pl.ds(k * span, span)
-        copies.append(pltpu.make_async_copy(table.at[neg_ids[k]], neg_t.at[:, lanes], sems.at[k]))
-    for b in range(chosen.shape[0]):
-        block = owners[b] * owned + locals_[b]
-        spot = neg_ids.shape[0] + b
-        copies.append(pltpu.make_async_copy(table.at[block], chosen.at[b], sems.at[spot]))
-    for copy in copies:
-        copy.start()
-    for copy in copies:
-        copy.wait()
-
-
-def run_pick(owners, locals_, neg_ids, table):
-    blocks, negs = owners.shape[0], neg_ids.shape[0]
-    width, span = table.shape[1:]
-    smem = pl.BlockSpec(memory_space=pltpu.SMEM)
-    vmem = pl.BlockSpec(memory_space=pltpu.VMEM)
-    anywhere = pl.BlockSpec(memory_space=pl.ANY)
-    return pl.pallas_call(
-        pick_blocks,
-        out_shape=(
-            jax.ShapeDtypeStruct((blocks, width, span), BF16),
-            jax.ShapeDtypeStruct((width, negs * span), BF16),
-        ),
-        in_specs=[smem, smem, smem, anywhere],
-        out_specs=(vmem, vmem),
-        scratch_shapes=[pltpu.SemaphoreType.DMA((blocks + negs,))],
-        compiler_params=pltpu.CompilerParams(vmem_limit_bytes=VMEM_BYTES),
-    )(owners, locals_, neg_ids, table)
+    )(owners, locals_, neg_ids, tail_t, head_t, rel_t, head_rows, relations)
 
 
 def remote(source, target, send_sem, recv_sem, device):
@@ -586,6 +573,23 @@
     )
     plane.start_first()
 
+    rows = hot_head.shape[0]
+    piece_rows = 160
+    for b in range(blocks):
+        hot_head[:, b * edges : (b + 1) * edges] = one_hot(rows, head_rows[b : b + 1, :])
+
+    def head_piece(p, squares):
+        spots = pl.ds(pl.multiple_of(p * piece_rows, piece_rows), piece_rows)
+        gradient = jnp.zeros((piece_rows, rows), F32)
+        for b in range(blocks):
+            lanes = slice(b * edges, (b + 1) * edges)
+            for n in range(2):
+                gradient = gradient + mm(grad[b, n, spots, :], hot_head[:, lanes], NT)
+        head_grad[spots, :] = gradient
+        return squares + jnp.sum(gradient * gradient, axis=0, keepdims=True)
+
+    squares = lax.fori_loop(0, width // piece_rows, head_piece, jnp.zeros((1, rows), F32))
+
     def spread_rows(piece):
         which, lanes = pieces[piece]
 
@@ -621,23 +625,10 @@
     high = PlaneSum(hi, hi_in_x, hi_in_y, hi_mid_x, hi_mid_y, hi_end_x, hi_end_y, (sem_hs, sem_hr))
     high.start_first()
     plane.start_second()
-
-    rows = hot_head.shape[0]
-    piece_rows = 160
-    for b in range(blocks):
-        hot_head[:, b * edges : (b + 1) * edges] = one_hot(rows, head_rows[b : b + 1, :])
-
-    def head_piece(p, squares):
-        spots = pl.ds(pl.multiple_of(p * piece_rows, piece_rows), piece_rows)
-        gradient = jnp.zeros((piece_rows, rows), F32)
-        for b in range(blocks):
-            lanes = slice(b * edges, (b + 1) * edges)
-            for n in range(2):
-                gradient = gradient + mm(grad[b, n, spots, :], hot_head[:, lanes], NT)
-        head_grad[spots, :] = gradient
-        return squares + jnp.sum(gradient * gradient, axis=0, keepdims=True)
-
-    squares = lax.fori_loop(0, width // piece_rows, head_piece, jnp.zeros((1, rows), F32))
+    arrive(2)
+    fill(lo, mm(seats[...], slot_rows[:, :CUT].astype(BF16)))
+    low = PlaneSum(lo, lo_in_x, lo_in_y, lo_mid_x, lo_mid_y, lo_end_x, lo_end_y, (sem_ls, sem_lr))
+    low.start_first()
 
     for place, total in enumerate(plane.result()):
         deep[place] = total
@@ -679,10 +670,22 @@
         def _():
             deep_copy(step).start()
 
-    arrive(2)
-    fill(lo, mm(seats[...], slot_rows[:, :CUT].astype(BF16)))
-    low = PlaneSum(lo, lo_in_x, lo_in_y, lo_mid_x, lo_mid_y, lo_end_x, lo_end_y, (sem_ls, sem_lr))
-    low.start_first()
+    high.start_second()
+
+    head_next = head_state[...] + squares / width
+    state_new[...] = head_next
+    rate = LEARN_RATE / jnp.sqrt(head_next)
+
+    @pl.loop(0, width // piece_rows)
+    def _(p):
+        spots = pl.ds(pl.multiple_of(p * piece_rows, piece_rows), piece_rows)
+        head_emb[spots, :] = (head_emb[spots, :].astype(F32) - head_grad[spots, :] * rate).astype(
+            BF16
+        )
+
+    head_store = pltpu.make_async_copy(head_emb, head_new, sem_local.at[6])
+    head_store.start()
+
     @pl.when(takes)
     def _():
         deep_in[depth] = deep[depth - zone * quarter]
@@ -701,22 +704,6 @@
         @pl.loop(1, TAIL)
         def _(step):
             total_copy(step).start()
-
-    high.start_second()
-
-    head_next = head_state[...] + squares / width
-    state_new[...] = head_next
-    rate = LEARN_RATE / jnp.sqrt(head_next)
-
-    @pl.loop(0, width // piece_rows)
-    def _(p):
-        spots = pl.ds(pl.multiple_of(p * piece_rows, piece_rows), piece_rows)
-        head_emb[spots, :] = (head_emb[spots, :].astype(F32) - head_grad[spots, :] * rate).astype(
-            BF16
-        )
-
-    head_store = pltpu.make_async_copy(head_emb, head_new, sem_local.at[6])
-    head_store.start()
 
     lane = lax.broadcasted_iota(jnp.int32, (group, span), 1)
     mark = lane == head * group + lax.broadcasted_iota(jnp.int32, (group, span), 0)
@@ -940,10 +927,9 @@
 ):
     owned, span, width = tail_emb.shape
     head_t, tail_t = head_emb.T, tail_emb.transpose(0, 2, 1)
-    table, query, rel_vec = gather_table(tail_t, head_t, relation_emb.T, head_rows, relations)
     owners = tail_owner.reshape(-1)
-    chosen, neg_t = run_pick(
-        owners, tail_local, neg_blocks, table.reshape(TAIL * owned, width, span)
+    query, rel_vec, chosen, neg_t = gather_table(
+        owners, tail_local, neg_blocks, tail_t, head_t, relation_emb.T, head_rows, relations
     )
     fresh, head_new, head_state_new = run_exchange(
         owners,

time: 134 us -> 128 us (0.955)
  Pallas kernels: 127 us -> 121 us
    pallas_call x1, Pallas kernels: 77.5 us -> 74.4 us  [run_exchange(): pl.pallas_call(exchange, out_shape=(jax.ShapeDtypeStruct((owned, HEAD, gr...]
    pallas_call x2 -> x1, Pallas kernels: 49.1 us -> 47 us  [gather_table(): pl.pallas_call(table_gather, out_shape=(jax.ShapeDtypeStruct((blocks, wid...]
where the time goes in v6:
time: 128 us
  Pallas kernels  121 us (95%)
  local copies, waits for them, and re-layouts  4.85 us (4%)
  between operations  1.31 us (1%)
    pallas_call x1, Pallas kernels, run_exchange(): pl.pallas_call(exchange, out_shape=(jax.ShapeDtypeStruct((owned, HEAD, gr...  74.4 us
    pallas_call x1, Pallas kernels, gather_table(): pl.pallas_call(table_gather, out_shape=(jax.ShapeDtypeStruct((blocks, wid...  47 us
    unnamed x8, local copies, waits for them, and re-layouts  3.78 us

profile of v6, /device:TPU:1, one launch (start us, length us, event | category | flops | bytes accessed | tf_op | source)
XLA Modules:
  0.0 128.1 jit_solution(11218822286536689961)
XLA Ops:
  1.3 47.0 %shard_map.147 = (bf16[4,800,256]{2,1,0:T(8,128)(2,1)}, bf16[4,800,256]{2,1,0:T(8,128)(2,1)}, bf16[4,800,128]{2,1,0:T(8,128)(2,1)}, bf16[800,1024]{1,0:T(8,128)(2,1)}) custom-call(s32[4]{0:T(128)} %bitcast.20, s32[4]{0:T(128)} %locals_.3, s32[8]{0:T(128)} %neg_ids.3, bf16[4,800,128]{2,1,0:T(8,128)(2,1)} %bitcast.11, bf16[800,512]{1,0:T(8,128)(2,1)} %bitcast.13, ...), custom_call_target="tpu_custom_call" | custom-call | tf_op jit(solution)/shard_map/pallas_call | solution.py:228
  48.3 74.4 %shard_map.148 = (bf16[4,16,8,896]{3,2,1,0:T(8,128)(2,1)}, bf16[800,512]{1,0:T(8,128)(2,1)}, f32[1,512]{1,0:T(1,128)}) custom-call(s32[4]{0:T(128)} %bitcast.21, s32[4]{0:T(128)} %locals_.3, s32[1]{0:T(128)S(6)} %copy.22.live_count, s32[8]{0:T(128)} %neg_ids.3, bf16[4,800,128]{2,1,0:T(8,128)(2,1)} %get-tuple-element.11.chosen_hbm, ...), custom_call_target="tpu_custom_call" | custom-call | tf_op jit(solution)/shard_map/pallas_call | solution.py:840
  122.6 0.0 copy-start
  122.6 1.1 slice.21
  123.7 0.1 copy.19
  123.8 0.6 fusion
  124.4 0.0 copy-start.1
  124.4 2.2 %copy.18 = bf16[4,128,800]{1,2,0:T(8,128)(2,1)} copy(bf16[4,128,800]{2,1,0:T(8,128)(2,1)} %bitcast.17) | data formatting | bytes 1638400
  126.6 0.0 copy-done
  126.6 0.9 copy.23
  127.5 0.0 copy-done.1
  127.5 0.6 copy.24
  (1 shorter events, 0.0 us)
Async XLA Ops:
  122.6 4.0 %copy-start = (bf16[800,512]{1,0:T(8,128)(2,1)S(1)}, bf16[800,512]{1,0:T(8,128)(2,1)}, u32[]{:S(2)}) copy-start(bf16[800,512]{1,0:T(8,128)(2,1)} %get-tuple-element.15) | copy-start | bytes 2457604
  124.4 3.1 %copy-start.1 = (f32[1,512]{1,0:T(1,128)S(1)}, f32[1,512]{1,0:T(1,128)}, u32[]{:S(2)}) copy-start(f32[1,512]{1,0:T(1,128)} %get-tuple-element.16) | copy-start | bytes 6148

commit v7 on v6

--- a/solution.py
+++ b/solution.py
@@ -321,11 +321,11 @@
             copy.wait_recv()
         for place in range(SIDE):
             for part in range(2):
-                total = spread[place, self.col, part]
-                other = spread[self.row, place, 2 + part]
+                total = spread[place, self.col, part].astype(F32)
+                other = spread[self.row, place, 2 + part].astype(F32)
                 for n in range(SIDE - 1):
-                    total = total + in_x[n, place, part]
-                    other = other + in_y[n, place, part]
+                    total = total + in_x[n, place, part].astype(F32)
+                    other = other + in_y[n, place, part].astype(F32)
                 mid_x[place, part] = total
                 mid_y[place, part] = other
         for copy in self.second():
@@ -505,7 +505,7 @@
 
     early = blocks // 2
     pieces = (
-        (pl.ds(0, early), pl.ds(0, LANES)),
+        *((pl.ds(b, 1), pl.ds(0, LANES)) for b in range(early)),
         (pl.ds(early, blocks - early), pl.ds(CUT, LANES - CUT)),
         (pl.ds(early, blocks - early), pl.ds(0, CUT)),
     )
@@ -521,21 +521,20 @@
             (peer, tail),
         )
 
-    @pl.loop(0, early)
-    def _(b):
+    for b in range(early):
         edge_block(b)
-
-    pl.semaphore_wait(barrier, HEAD + TAIL - 2)
-
-    @pl.loop(1, HEAD)
-    def _(step):
-        block_copy(0, step).start()
+        if b == 0:
+            pl.semaphore_wait(barrier, HEAD + TAIL - 2)
+
+        @pl.loop(1, HEAD)
+        def _(step):
+            block_copy(b, step).start()
 
     @pl.loop(early, blocks)
     def _(b):
         edge_block(b)
 
-    for piece in (1, 2):
+    for piece in range(early, len(pieces)):
 
         @pl.loop(1, HEAD)
         def _(step):
@@ -567,7 +566,8 @@
     for part in range(SIDE):
         pair_copy(part).wait_recv()
         for place in range(SIDE):
-            mine[part, place] = neg_part[part, place, :, core] + theirs[part, place]
+            total = neg_part[part, place, :, core] + theirs[part, place]
+            mine[part, place] = total.astype(BF16)
     plane = PlaneSum(
         mine, neg_in_x, neg_in_y, neg_mid_x, neg_mid_y, neg_end_x, neg_end_y, (sem_ps, sem_pr)
     )
@@ -613,8 +613,8 @@
             y, x, part = block // owned // SIDE, block // owned % SIDE, block % owned
             dense[y, x, part] = sums[block * group : (block + 1) * group]
 
-    arrive(0)
-    arrive(1)
+    for piece in range(len(pieces) - 1):
+        arrive(piece)
     count = HEAD * owned * group
     number = slot_rows[:, width : width + 1]
     inner = lax.broadcasted_iota(jnp.int32, (count, 1), 0) % group
@@ -625,7 +625,7 @@
     high = PlaneSum(hi, hi_in_x, hi_in_y, hi_mid_x, hi_mid_y, hi_end_x, hi_end_y, (sem_hs, sem_hr))
     high.start_first()
     plane.start_second()
-    arrive(2)
+    arrive(len(pieces) - 1)
     fill(lo, mm(seats[...], slot_rows[:, :CUT].astype(BF16)))
     low = PlaneSum(lo, lo_in_x, lo_in_y, lo_mid_x, lo_mid_y, lo_end_x, lo_end_y, (sem_ls, sem_lr))
     low.start_first()
@@ -767,7 +767,7 @@
     for part in range(SIDE):
         pair_copy(part).wait_send()
 
-    for piece in range(3):
+    for piece in range(len(pieces)):
 
         @pl.loop(1, HEAD)
         def _(step):
@@ -829,10 +829,10 @@
     anywhere = pl.BlockSpec(memory_space=pl.ANY)
     vmem = pl.BlockSpec(memory_space=pltpu.VMEM)
 
-    def plane_sum(columns):
+    def plane_sum(columns, sent=F32):
         return [
-            pltpu.VMEM((SIDE, SIDE, 4, group, columns), F32),
-            *([pltpu.VMEM((SIDE - 1, SIDE, 2, group, columns), F32)] * 2),
+            pltpu.VMEM((SIDE, SIDE, 4, group, columns), sent),
+            *([pltpu.VMEM((SIDE - 1, SIDE, 2, group, columns), sent)] * 2),
             *([pltpu.VMEM((SIDE, 2, group, columns), F32)] * 2),
             *([pltpu.VMEM((SIDE - 1, 2, group, columns), F32)] * 2),
         ]
@@ -861,7 +861,7 @@
             pltpu.VMEM((SIDE, SIDE, 4, 2, group, width), F32),
             pltpu.VMEM((HEAD, owned, group, LANES), BF16),
             pltpu.VMEM((SIDE, SIDE, 4, group, width), F32),
-            *plane_sum(width),
+            *plane_sum(width, BF16),
             pltpu.VMEM((quarter, group, width), F32),
             pltpu.VMEM((DEPTH, group, width), F32),
             pltpu.VMEM((negs, group, width), F32),
@@ -870,8 +870,8 @@
             *plane_sum(CUT),
             *plane_sum(width - CUT),
             pltpu.VMEM((owned, group, LANES), BF16),
-            sems((3, HEAD)),
-            sems((3, HEAD)),
+            sems((blocks // 2 + 2, HEAD)),
+            sems((blocks // 2 + 2, HEAD)),
             sems((SIDE,)),
             sems((SIDE,)),
             sems((12,)),

time: 128 us -> 123 us (0.961)
  Pallas kernels: 121 us -> 116 us
    pallas_call x1, Pallas kernels: 74.4 us -> 68.8 us  [run_exchange(): pl.pallas_call(exchange, out_shape=(jax.ShapeDtypeStruct((owned, HEAD, gr...]
where the time goes in v7:
time: 123 us
  Pallas kernels  116 us (94%)
  local copies, waits for them, and re-layouts  4.85 us (4%)
  between operations  1.31 us (1%)
    pallas_call x1, Pallas kernels, run_exchange(): pl.pallas_call(exchange, out_shape=(jax.ShapeDtypeStruct((owned, HEAD, gr...  68.8 us
    pallas_call x1, Pallas kernels, gather_table(): pl.pallas_call(table_gather, out_shape=(jax.ShapeDtypeStruct((blocks, wid...  47 us
    unnamed x8, local copies, waits for them, and re-layouts  3.78 us

profile of v7, /device:TPU:1, one launch (start us, length us, event | category | flops | bytes accessed | tf_op | source)
XLA Modules:
  0.0 122.6 jit_solution(15839421094066163814)
XLA Ops:
  1.3 47.0 %shard_map.147 = (bf16[4,800,256]{2,1,0:T(8,128)(2,1)}, bf16[4,800,256]{2,1,0:T(8,128)(2,1)}, bf16[4,800,128]{2,1,0:T(8,128)(2,1)}, bf16[800,1024]{1,0:T(8,128)(2,1)}) custom-call(s32[4]{0:T(128)} %bitcast.20, s32[4]{0:T(128)} %locals_.3, s32[8]{0:T(128)} %neg_ids.3, bf16[4,800,128]{2,1,0:T(8,128)(2,1)} %bitcast.11, bf16[800,512]{1,0:T(8,128)(2,1)} %bitcast.13, ...), custom_call_target="tpu_custom_call" | custom-call | tf_op jit(solution)/shard_map/pallas_call | solution.py:228
  48.3 68.8 %shard_map.148 = (bf16[4,16,8,896]{3,2,1,0:T(8,128)(2,1)}, bf16[800,512]{1,0:T(8,128)(2,1)}, f32[1,512]{1,0:T(1,128)}) custom-call(s32[4]{0:T(128)} %bitcast.21, s32[4]{0:T(128)} %locals_.3, s32[1]{0:T(128)S(6)} %copy.22.live_count, s32[8]{0:T(128)} %neg_ids.3, bf16[4,800,128]{2,1,0:T(8,128)(2,1)} %get-tuple-element.11.chosen_hbm, ...), custom_call_target="tpu_custom_call" | custom-call | tf_op jit(solution)/shard_map/pallas_call | solution.py:840
  117.1 0.0 copy-start
  117.1 1.1 slice.21
  118.2 0.1 copy.19
  118.3 0.6 fusion
  118.9 0.0 copy-start.1
  118.9 2.2 %copy.18 = bf16[4,128,800]{1,2,0:T(8,128)(2,1)} copy(bf16[4,128,800]{2,1,0:T(8,128)(2,1)} %bitcast.17) | data formatting | bytes 1638400
  121.1 0.0 copy-done
  121.1 0.9 copy.23
  122.0 0.0 copy-done.1
  122.0 0.6 copy.24
  (1 shorter events, 0.0 us)
Async XLA Ops:
  117.1 4.0 %copy-start = (bf16[800,512]{1,0:T(8,128)(2,1)S(1)}, bf16[800,512]{1,0:T(8,128)(2,1)}, u32[]{:S(2)}) copy-start(bf16[800,512]{1,0:T(8,128)(2,1)} %get-tuple-element.15) | copy-start | bytes 2457604
  118.9 3.1 %copy-start.1 = (f32[1,512]{1,0:T(1,128)S(1)}, f32[1,512]{1,0:T(1,128)}, u32[]{:S(2)}) copy-start(f32[1,512]{1,0:T(1,128)} %get-tuple-element.16) | copy-start | bytes 6148

commit v8 on v7

--- a/solution.py
+++ b/solution.py
@@ -321,11 +321,11 @@
             copy.wait_recv()
         for place in range(SIDE):
             for part in range(2):
-                total = spread[place, self.col, part].astype(F32)
-                other = spread[self.row, place, 2 + part].astype(F32)
+                total = spread[place, self.col, part]
+                other = spread[self.row, place, 2 + part]
                 for n in range(SIDE - 1):
-                    total = total + in_x[n, place, part].astype(F32)
-                    other = other + in_y[n, place, part].astype(F32)
+                    total = total + in_x[n, place, part]
+                    other = other + in_y[n, place, part]
                 mid_x[place, part] = total
                 mid_y[place, part] = other
         for copy in self.second():
@@ -567,7 +567,7 @@
         pair_copy(part).wait_recv()
         for place in range(SIDE):
             total = neg_part[part, place, :, core] + theirs[part, place]
-            mine[part, place] = total.astype(BF16)
+            mine[part, place] = total
     plane = PlaneSum(
         mine, neg_in_x, neg_in_y, neg_mid_x, neg_mid_y, neg_end_x, neg_end_y, (sem_ps, sem_pr)
     )
@@ -829,10 +829,10 @@
     anywhere = pl.BlockSpec(memory_space=pl.ANY)
     vmem = pl.BlockSpec(memory_space=pltpu.VMEM)
 
-    def plane_sum(columns, sent=F32):
+    def plane_sum(columns):
         return [
-            pltpu.VMEM((SIDE, SIDE, 4, group, columns), sent),
-            *([pltpu.VMEM((SIDE - 1, SIDE, 2, group, columns), sent)] * 2),
+            pltpu.VMEM((SIDE, SIDE, 4, group, columns), F32),
+            *([pltpu.VMEM((SIDE - 1, SIDE, 2, group, columns), F32)] * 2),
             *([pltpu.VMEM((SIDE, 2, group, columns), F32)] * 2),
             *([pltpu.VMEM((SIDE - 1, 2, group, columns), F32)] * 2),
         ]
@@ -861,7 +861,7 @@
             pltpu.VMEM((SIDE, SIDE, 4, 2, group, width), F32),
             pltpu.VMEM((HEAD, owned, group, LANES), BF16),
             pltpu.VMEM((SIDE, SIDE, 4, group, width), F32),
-            *plane_sum(width, BF16),
+            *plane_sum(width),
             pltpu.VMEM((quarter, group, width), F32),
             pltpu.VMEM((DEPTH, group, width), F32),
             pltpu.VMEM((negs, group, width), F32),

time: 123 us -> 128 us (1.041)
  Pallas kernels: 116 us -> 120 us
    pallas_call x1, Pallas kernels: 68.8 us -> 72.6 us  [run_exchange(): pl.pallas_call(exchange, out_shape=(jax.ShapeDtypeStruct((owned, HEAD, gr...]
where the time goes in v8:
time: 128 us; the launch traced here: 126 us
  Pallas kernels  120 us (94%)
  local copies, waits for them, and re-layouts  4.85 us (4%)
  between operations  1.31 us (1%)
    pallas_call x1, Pallas kernels, run_exchange(): pl.pallas_call(exchange, out_shape=(jax.ShapeDtypeStruct((owned, HEAD, gr...  72.6 us
    pallas_call x1, Pallas kernels, gather_table(): pl.pallas_call(table_gather, out_shape=(jax.ShapeDtypeStruct((blocks, wid...  47 us
    unnamed x8, local copies, waits for them, and re-layouts  3.78 us

profile of v8, /device:TPU:1, one launch (start us, length us, event | category | flops | bytes accessed | tf_op | source)
XLA Modules:
  0.0 126.3 jit_solution(16459836810727649686)
XLA Ops:
  1.3 47.0 %shard_map.147 = (bf16[4,800,256]{2,1,0:T(8,128)(2,1)}, bf16[4,800,256]{2,1,0:T(8,128)(2,1)}, bf16[4,800,128]{2,1,0:T(8,128)(2,1)}, bf16[800,1024]{1,0:T(8,128)(2,1)}) custom-call(s32[4]{0:T(128)} %bitcast.20, s32[4]{0:T(128)} %locals_.3, s32[8]{0:T(128)} %neg_ids.3, bf16[4,800,128]{2,1,0:T(8,128)(2,1)} %bitcast.11, bf16[800,512]{1,0:T(8,128)(2,1)} %bitcast.13, ...), custom_call_target="tpu_custom_call" | custom-call | tf_op jit(solution)/shard_map/pallas_call | solution.py:228
  48.3 72.6 %shard_map.148 = (bf16[4,16,8,896]{3,2,1,0:T(8,128)(2,1)}, bf16[800,512]{1,0:T(8,128)(2,1)}, f32[1,512]{1,0:T(1,128)}) custom-call(s32[4]{0:T(128)} %bitcast.21, s32[4]{0:T(128)} %locals_.3, s32[1]{0:T(128)S(6)} %copy.22.live_count, s32[8]{0:T(128)} %neg_ids.3, bf16[4,800,128]{2,1,0:T(8,128)(2,1)} %get-tuple-element.11.chosen_hbm, ...), custom_call_target="tpu_custom_call" | custom-call | tf_op jit(solution)/shard_map/pallas_call | solution.py:840
  120.8 0.0 copy-start
  120.9 1.1 slice.21
  121.9 0.1 copy.19
  122.1 0.6 fusion
  122.6 0.0 copy-start.1
  122.7 2.2 %copy.18 = bf16[4,128,800]{1,2,0:T(8,128)(2,1)} copy(bf16[4,128,800]{2,1,0:T(8,128)(2,1)} %bitcast.17) | data formatting | bytes 1638400
  124.8 0.0 copy-done
  124.8 0.9 copy.23
  125.7 0.0 copy-done.1
  125.7 0.6 copy.24
  (1 shorter events, 0.0 us)
Async XLA Ops:
  120.8 4.0 %copy-start = (bf16[800,512]{1,0:T(8,128)(2,1)S(1)}, bf16[800,512]{1,0:T(8,128)(2,1)}, u32[]{:S(2)}) copy-start(bf16[800,512]{1,0:T(8,128)(2,1)} %get-tuple-element.15) | copy-start | bytes 2457604
  122.6 3.1 %copy-start.1 = (f32[1,512]{1,0:T(1,128)S(1)}, f32[1,512]{1,0:T(1,128)}, u32[]{:S(2)}) copy-start(f32[1,512]{1,0:T(1,128)} %get-tuple-element.16) | copy-start | bytes 6148
